TPU v7x, 32 devices: a whole 2x2x4 slice. The times are simulated.
32 devices in a mesh: wide: 2 (over x), narrow: 4 (over y, core), seq: 4 (over z).
Axes of the slice: x: 2, y: 2, z: 4, core: 2. Of those that a mesh axis runs over, the one named last changes fastest.
Arguments:
- attn_query: bfloat16 [1024, 73728], P(('seq', 'wide'), 'narrow'), parts along dimension 0, may hold values from -6 to 6
- key_latent: bfloat16 [1024, 576], P(('seq', 'wide')), parts along dimension 0, may hold values from -6 to 6
- lse_attn: float32 [128, 1024], P('narrow', ('seq', 'wide')), parts along dimension 1, may hold values from 1 to 3
- index_query: bfloat16 [1024, 8192], P(('seq', 'wide'), 'narrow'), parts along dimension 0, may hold values from -6 to 6
- index_key: bfloat16 [1024, 128], P(('seq', 'wide')), parts along dimension 0, may hold values from -6 to 6
- index_weight: float32 [64, 1024], P('narrow', ('seq', 'wide')), parts along dimension 1, may hold values from -0.75 to 0.75
- lse_index: float32 [1024], P(('seq', 'wide')), parts along dimension 0, may hold values from 0 to 1
- block_order: int32 [8], P('seq'), parts along dimension 0, may hold values from 0 to 127, as said below
Outputs:
- d_index_query: float32 [1024, 8192], P(('seq', 'wide'), 'narrow'), parts along dimension 0
- d_index_weight: float32 [64, 1024], P('narrow', ('seq', 'wide')), parts along dimension 1
- d_index_key: float32 [1024, 128], P(('seq', 'wide')), parts along dimension 0
There are 4 independent parts, one for each index of `seq`. A program takes and returns all parts, laid end to end along the dimension named above; each array names one. Nothing has to cross between parts.
Inputs may be any that keep to these rules, and one draw needn't show every extreme that they name: Index d of wide holds tokens 128 * block_order[d] to 128 * block_order[d] + 127 of the context; the values are distinct.
All inputs are finite; a program needn't handle non-finite values.
Results may differ from a plain program's by a relative error of at most 0.008.
Values may be sent and summed in bfloat16 or wider, within the bound.
No kernel may reach another device: no remote copies, remote signals or barrier semaphores. Data moves between devices by JAX's collectives and lax.ppermute only.
A program may use at most 64 MiB of HBM per device.

v0:
```python
import jax
import jax.numpy as jnp
from jax import lax
from jax.sharding import PartitionSpec as P

HEADS = 128


attn_scale = 192.0 ** (-0.5)


def shifted(block, axis, distance):
    devices = range(lax.axis_size(axis))
    route = [((i - distance) % len(devices), i) for i in devices]
    return lax.ppermute(block, axis, route)


def body(
    attn_query, key_latent, lse_attn, index_query, index_key, index_weight, lse_index, block_order
):
    tok_rows = key_latent.shape[0]
    key_width = key_latent.shape[1]
    index_width = index_key.shape[1]
    heads_here = attn_query.shape[1] // key_width
    iheads_here = index_query.shape[1] // index_width
    cycle_size = lax.axis_size("wide")
    cycle_place = lax.axis_index("wide")
    query_heads = attn_query.reshape(tok_rows, heads_here, key_width)
    index_heads = index_query.reshape(tok_rows, iheads_here, index_width)
    offsets = jnp.arange(tok_rows, dtype=jnp.int32)
    query_pos = block_order[cycle_place] * tok_rows + offsets
    lse_rows = jnp.transpose(lse_attn)
    weight_rows = jnp.transpose(index_weight)
    index_scale = index_width ** (-0.5)

    def block_grads(key_block, ikey_block, source):
        key_pos = block_order[source] * tok_rows + offsets
        causal = query_pos[:, None] >= key_pos[None, :]
        scores = (
            jnp.einsum("thc,sc->ths", query_heads, key_block, preferred_element_type=jnp.float32)
            * attn_scale
        )
        part_target = jnp.sum(jnp.exp(scores - lse_rows[:, :, None]), axis=1) / HEADS
        logits = (
            jnp.einsum("tjc,sc->tjs", index_heads, ikey_block, preferred_element_type=jnp.float32)
            * index_scale
        )
        active = jnp.maximum(logits, 0.0)
        part_score = jnp.einsum("tjs,tj->ts", active, weight_rows)
        target, score = lax.psum((part_target, part_score), "narrow")
        difference = jnp.where(causal, jnp.exp(score - lse_index[:, None]) - target, 0.0)
        grad_weight = jnp.einsum("ts,tjs->tj", difference, active)
        coefficient = (
            difference[:, None, :]
            * weight_rows[:, :, None]
            * (logits > 0.0).astype(jnp.float32)
            * index_scale
        ).astype(jnp.bfloat16)
        grad_query = jnp.einsum(
            "tjs,sc->tjc", coefficient, ikey_block, preferred_element_type=jnp.float32
        )
        grad_key = jnp.einsum(
            "tjs,tjc->sc", coefficient, index_heads, preferred_element_type=jnp.float32
        )
        return (grad_query, grad_weight, grad_key)

    def move_keys(key_block, ikey_block):
        return shifted((key_block, ikey_block), "wide", 1)

    zero_query = jnp.zeros((tok_rows, iheads_here, index_width), jnp.float32)
    zero_weight = jnp.zeros((tok_rows, iheads_here), jnp.float32)
    last_source = (cycle_place + 1) % cycle_size

    def pass_grad(carried):
        return shifted(carried, "wide", 1)

    def cycle_step(step_index, carried_state):
        key_block, ikey_block, carried, sum_query, sum_weight = carried_state
        source = (cycle_place - step_index) % cycle_size
        grad_query, grad_weight, grad_key = block_grads(key_block, ikey_block, source)
        key_block, ikey_block = move_keys(key_block, ikey_block)
        return (
            key_block,
            ikey_block,
            pass_grad(carried + grad_key),
            sum_query + grad_query,
            sum_weight + grad_weight,
        )

    start_state = (
        key_latent,
        index_key,
        jnp.zeros((tok_rows, index_width), jnp.float32),
        zero_query,
        zero_weight,
    )
    key_block, ikey_block, carried, sum_query, sum_weight = lax.fori_loop(
        0, cycle_size - 1, cycle_step, start_state
    )
    grad_query, grad_weight, grad_key = block_grads(key_block, ikey_block, last_source)
    own_key = pass_grad(carried + grad_key)
    key_total = lax.psum(own_key, "narrow")
    sum_query = sum_query + grad_query
    sum_weight = sum_weight + grad_weight
    return (
        sum_query.reshape(tok_rows, iheads_here * index_width),
        jnp.transpose(sum_weight),
        key_total,
    )


def solution(mesh):
    in_specs = (
        P(("seq", "wide"), "narrow"),
        P(("seq", "wide"), None),
        P("narrow", ("seq", "wide")),
        P(("seq", "wide"), "narrow"),
        P(("seq", "wide"), None),
        P("narrow", ("seq", "wide")),
        P(("seq", "wide")),
        P("seq"),
    )
    out_specs = (
        P(("seq", "wide"), "narrow"),
        P("narrow", ("seq", "wide")),
        P(("seq", "wide"), None),
    )
    return jax.shard_map(body, mesh=mesh, in_specs=in_specs, out_specs=out_specs, check_vma=False)
```

profile of v0, /device:TPU:0, one launch (start us, length us, event | category | flops | bytes accessed | tf_op | source)
XLA Modules:
  0.0 119.6 jit_solution(2977630586859763670)
XLA Ops:
  7.2 0.0 copy-start
  7.2 0.0 all-reduce.6.cloned.1.call-start
  7.2 3.0 %collective-permute-start = (bf16[128,128]{1,0:T(8,128)(2,1)}, bf16[128,128]{1,0:T(8,128)(2,1)S(1)}, u32[]{:S(2)}, u32[]{:S(2)}) collective-permute-start(bf16[128,128]{1,0:T(8,128)(2,1)} %param.12), channel_id=1, source_target_pairs={{16,0},{0,16},{17,1},{1,17},{18,2},{2,18},{19,3},{3,19},{20,4},{4,... | collective-permute-start | bytes 98312 | tf_op jit(solution)/shard_map/while/body/eval_jaxpr/ppermute | solution.py:15
  10.3 0.1 collective-permute-start.1
  10.3 1.4 %fusion.43 = (s32[1]{0:T(128)}, s32[1]{0:T(128)}, s32[1]{0:T(128)}) fusion(s32[2]{0:T(128)} %param.15, s32[]{:T(128)S(6)} %select_n.36, s32[]{:T(128)S(6)} %select_n.31, s32[]{:T(128)S(6)} %select_n.33), kind=kLoop, calls=%fused_computation.67 | loop fusion | bytes 36 | tf_op jit(solution)/shard_map/dynamic_slice | solution.py:37
  13.6 0.8 copy.33
  14.5 0.0 copy-done
  14.5 1.1 broadcast_maximum_fusion.1
  15.6 0.1 fusion.9
  15.7 0.0 copy-start.5
  15.7 0.0 copy-start.6
  15.7 6.7 %copy.23 = bf16[128,18432]{0,1:T(8,128)(2,1)} copy(bf16[128,18432]{1,0:T(8,128)(2,1)} %param.8) | data formatting | bytes 9437184 | tf_op args[0]
  22.4 0.0 slice-start
  22.4 0.0 copy-done.5
  22.4 0.0 copy-done.6
  22.4 0.0 slice-start.1
  22.4 4.5 %exponential_reduce_fusion.1 = f32[128,128]{1,0:T(8,128)S(1)} fusion(bf16[128,32,576]{0,2,1:T(8,128)(2,1)} %bitcast.87, f32[128,32]{0,1:T(8,128)S(1)} %bitcast.101, bf16[128,576]{0,1:T(8,128)(2,1)S(1)} %copy-done.5), kind=kOutput, calls=%fused_computation.1 | convolution fusion | flops 605536256 | bytes 4947968 | tf_op jit(solution)/shard_map/while/body/eval_jaxpr/thc,sc->ths/dot_general | solution.py:40
  26.9 0.6 broadcast_multiply_fusion.1
  27.6 1.1 fusion.7
  28.6 0.0 collective-permute-done
  28.6 0.3 broadcast_maximum_fusion
  29.0 1.1 fusion.3
  30.0 0.0 copy-start.4
  30.0 0.0 copy-start.3
  30.0 0.0 collective-permute-done.1
  30.0 0.0 slice-done
  30.0 0.0 slice-done.1
  30.0 2.2 %exponential_reduce_fusion = f32[128,128]{1,0:T(8,128)S(1)} fusion(bf16[128,32,576]{0,2,1:T(8,128)(2,1)S(1)} %bitcast.90, f32[128,32]{0,1:T(8,128)S(1)} %bitcast.102, bf16[128,576]{0,1:T(8,128)(2,1)S(1)} %collective-permute-done.1), kind=kOutput, calls=%fused_computation | convolution fusion | flops 605536256 | bytes 4947968 | tf_op jit(solution)/shard_map/thc,sc->ths/dot_general | solution.py:40
  32.2 0.6 broadcast_multiply_fusion
  32.8 0.0 all-reduce.6.cloned.1.call-update
  32.9 0.0 all-reduce.4.cloned.1.call-start
  32.9 0.0 copy-start.2
  32.9 0.1 fusion.10
  33.1 34.1 %all-reduce.6.cloned.1.call-done = (f32[128,128]{1,0:T(8,128)}, f32[128,128]{1,0:T(8,128)}, f32[128,128]{1,0:T(8,128)}, f32[128,128]{1,0:T(8,128)}) async-done(((f32[128,128]{1,0:T(8,128)}, f32[128,128]{1,0:T(8,128)}, f32[128,128]{1,0:T(8,128)}, f32[128,128]{1,0:T(8,128)}), (f32[128,128]{1,0:T(8,128)}, f32[128,128]{1,0:T(8,128)}, f32[128,128]{1,0:T(8,128)}, ...) | async-done | bytes 262160 | tf_op jit(solution)/shard_map/while/body/eval_jaxpr/psum | solution.py:50
  67.2 0.0 copy-done.4
  67.2 1.0 subtract_select_fusion
  68.3 0.0 copy-done.3
  68.3 0.7 convolution_bitcast_fusion.1
  69.0 0.0 copy-done.2
  69.0 0.6 fusion.15
  69.6 1.5 %collective-permute-start.2 = (f32[128,128]{1,0:T(8,128)S(1)}, f32[128,128]{1,0:T(8,128)S(1)}, u32[]{:S(2)}, u32[]{:S(2)}) collective-permute-start(f32[128,128]{1,0:T(8,128)S(1)} %convolution_bitcast_fusion.1), channel_id=1, source_target_pairs={{16,0},{0,16},{17,1},{1,17},{18,2},{2,18},{19,3},{3,19},{20,4},{4,... | collective-permute-start | bytes 196616 | tf_op jit(solution)/shard_map/while/body/eval_jaxpr/ppermute | solution.py:15
  71.1 0.6 convolution_add_fusion
  71.7 0.4 fusion.1
  72.1 1.8 %collective-permute-done.2 = f32[128,128]{1,0:T(8,128)S(1)} collective-permute-done((f32[128,128]{1,0:T(8,128)S(1)}, f32[128,128]{1,0:T(8,128)S(1)}, u32[]{:S(2)}, u32[]{:S(2)}) %collective-permute-start.2) | collective-permute-done | bytes 65568 | tf_op jit(solution)/shard_map/while/body/eval_jaxpr/ppermute | solution.py:15
  73.9 0.7 fusion
  74.6 1.5 %collective-permute-start.3 = (f32[128,128]{1,0:T(8,128)S(1)}, f32[128,128]{1,0:T(8,128)S(1)}, u32[]{:S(2)}, u32[]{:S(2)}) collective-permute-start(f32[128,128]{1,0:T(8,128)S(1)} %fusion), channel_id=1, source_target_pairs={{16,0},{0,16},{17,1},{1,17},{18,2},{2,18},{19,3},{3,19},{20,4},{4,... | collective-permute-start | bytes 196616 | tf_op jit(solution)/shard_map/ppermute | solution.py:15
  76.2 0.4 fusion.5
  76.6 0.1 copy.42
  76.7 0.1 copy.40
  76.7 2.2 %collective-permute-done.3 = f32[128,128]{1,0:T(8,128)S(1)} collective-permute-done((f32[128,128]{1,0:T(8,128)S(1)}, f32[128,128]{1,0:T(8,128)S(1)}, u32[]{:S(2)}, u32[]{:S(2)}) %collective-permute-start.3) | collective-permute-done | bytes 65568 | tf_op jit(solution)/shard_map/ppermute | solution.py:15
  79.0 0.0 copy-start.1
  79.0 0.6 copy-done.1
  79.6 0.0 all-reduce.4.cloned.1.call-update
  79.6 0.6 fusion.30
  80.2 1.3 %copy.31 = f32[128,2048]{1,0:T(8,128)} copy(f32[128,2048]{0,1:T(8,128)S(1)} %bitcast.91) | data formatting | bytes 2097152
  81.5 29.8 %all-reduce.4.cloned.1.call-done = f32[128,128]{1,0:T(8,128)} async-done(((f32[128,128]{1,0:T(8,128)}), f32[128,128]{1,0:T(8,128)}) %all-reduce.4.cloned.1.call-update) | async-done | bytes 65552 | tf_op jit(solution)/shard_map/psum | solution.py:102
  111.3 1.5 %copy.82 = f32[128,128]{1,0:T(8,128)} copy(f32[128,128]{1,0:T(8,128)} %all-reduce.4.cloned.1.call-done) | data formatting | bytes 131072
  (3 shorter events, 0.0 us)
Async XLA Ops:
  7.2 7.3 %copy-start = (bf16[128,2048]{1,0:T(8,128)(2,1)S(1)}, bf16[128,2048]{1,0:T(8,128)(2,1)}, u32[]{:S(2)}) copy-start(bf16[128,2048]{1,0:T(8,128)(2,1)} %param.11) | copy-start | bytes 1572868
  7.2 60.0 %all-reduce.6.cloned.1.call-start = ((), (), s32[]{:S(2)}) async-start(), calls=%async_computation.1 | async-start | bytes 524288 | tf_op jit(solution)/shard_map/while/body/eval_jaxpr/psum | solution.py:50
  7.2 21.4 %collective-permute-start = (bf16[128,128]{1,0:T(8,128)(2,1)}, bf16[128,128]{1,0:T(8,128)(2,1)S(1)}, u32[]{:S(2)}, u32[]{:S(2)}) collective-permute-start(bf16[128,128]{1,0:T(8,128)(2,1)} %param.12), channel_id=1, source_target_pairs={{16,0},{0,16},{17,1},{1,17},{18,2},{2,18},{19,3},{3,19},{20,4},{4,... | collective-permute-start | bytes 98312 | tf_op jit(solution)/shard_map/while/body/eval_jaxpr/ppermute | solution.py:15
  10.3 19.8 %collective-permute-start.1 = (bf16[128,576]{0,1:T(8,128)(2,1)}, bf16[128,576]{0,1:T(8,128)(2,1)S(1)}, u32[]{:S(2)}, u32[]{:S(2)}) collective-permute-start(bf16[128,576]{0,1:T(8,128)(2,1)} %param.9), channel_id=1, source_target_pairs={{16,0},{0,16},{17,1},{1,17},{18,2},{2,18},{19,3},{3,19},{20,4},{4,... | collective-permute-start | bytes 442376 | tf_op jit(solution)/shard_map/while/body/eval_jaxpr/ppermute | solution.py:15
  15.7 6.7 %copy-start.5 = (bf16[128,576]{0,1:T(8,128)(2,1)S(1)}, bf16[128,576]{0,1:T(8,128)(2,1)}, u32[]{:S(2)}) copy-start(bf16[128,576]{0,1:T(8,128)(2,1)} %param.9) | copy-start | bytes 442372
  15.7 6.7 %copy-start.6 = (f32[32,128]{1,0:T(8,128)S(1)}, f32[32,128]{1,0:T(8,128)}, u32[]{:S(2)}) copy-start(f32[32,128]{1,0:T(8,128)} %param.10) | copy-start | bytes 49156
  22.4 7.6 %slice-start = ((s8[4718592]{0:T(1024)(128)(4,1)}), s8[4194304]{0:T(1024)(128)(4,1)S(1)}, s32[]{:S(2)}) async-start(s8[4718592]{0:T(1024)(128)(4,1)} %bitcast.88), calls=%async_computation.2 | async-start | bytes 8388608
  22.4 7.6 %slice-start.1 = ((s8[4718592]{0:T(1024)(128)(4,1)}), s8[524288]{0:T(1024)(128)(4,1)S(1)}, s32[]{:S(2)}) async-start(s8[4718592]{0:T(1024)(128)(4,1)} %bitcast.88), calls=%async_computation.3 | async-start | bytes 1048576
  30.0 37.2 %copy-start.4 = (f32[128]{0:T(128)S(1)}, f32[128]{0:T(128)}, u32[]{:S(2)}) copy-start(f32[128]{0:T(128)} %param.14) | copy-start | bytes 1540
  30.0 38.3 %copy-start.3 = (f32[16,128]{1,0:T(8,128)S(1)}, f32[16,128]{1,0:T(8,128)}, u32[]{:S(2)}) copy-start(f32[16,128]{1,0:T(8,128)} %param.13) | copy-start | bytes 24580
  32.9 78.4 %all-reduce.4.cloned.1.call-start = ((), (), s32[]{:S(2)}) async-start(), calls=%async_computation | async-start | bytes 131072 | tf_op jit(solution)/shard_map/psum | solution.py:102
  32.9 36.1 %copy-start.2 = (bf16[128,128]{1,0:T(8,128)(2,1)S(1)}, bf16[128,128]{1,0:T(8,128)(2,1)}, u32[]{:S(2)}) copy-start(bf16[128,128]{1,0:T(8,128)(2,1)} %param.12) | copy-start | bytes 98308
  69.6 4.3 %collective-permute-start.2 = (f32[128,128]{1,0:T(8,128)S(1)}, f32[128,128]{1,0:T(8,128)S(1)}, u32[]{:S(2)}, u32[]{:S(2)}) collective-permute-start(f32[128,128]{1,0:T(8,128)S(1)} %convolution_bitcast_fusion.1), channel_id=1, source_target_pairs={{16,0},{0,16},{17,1},{1,17},{18,2},{2,18},{19,3},{3,19},{20,4},{4,... | collective-permute-start | bytes 196616 | tf_op jit(solution)/shard_map/while/body/eval_jaxpr/ppermute | solution.py:15
  74.6 4.3 %collective-permute-start.3 = (f32[128,128]{1,0:T(8,128)S(1)}, f32[128,128]{1,0:T(8,128)S(1)}, u32[]{:S(2)}, u32[]{:S(2)}) collective-permute-start(f32[128,128]{1,0:T(8,128)S(1)} %fusion), channel_id=1, source_target_pairs={{16,0},{0,16},{17,1},{1,17},{18,2},{2,18},{19,3},{3,19},{20,4},{4,... | collective-permute-start | bytes 196616 | tf_op jit(solution)/shard_map/ppermute | solution.py:15
  79.0 0.6 copy-start.1
Sparse Core Ops, SparseCore 0:
  33.0 34.1 all-reduce.5
  79.7 31.5 all-reduce.3
where the time goes:
time: 120 us
  waiting for transfers between devices  67.9 us (57%)
  between operations  16.2 us (14%)
  matrix products  13.6 us (11%)
  local copies, waits for them, and re-layouts  12.4 us (10%)
  starting transfers between devices  6.27 us (5%)
  other arithmetic  3.2 us (3%)
    psum x1, waiting for transfers between devices, block_grads(): target, score = lax.psum((part_target, part_score), 'narrow')  34.1 us
    psum x1, waiting for transfers between devices, body(): key_total = lax.psum(own_key, 'narrow')  29.8 us
    unnamed x21, local copies, waits for them, and re-layouts  10.1 us
    dot_general x2, matrix products, block_grads(): jnp.einsum('thc,sc->ths', query_heads, key_block, preferred_element_type=...  6.66 us
    ppermute x4, starting transfers between devices, shifted(): return lax.ppermute(block, axis, route)  6.19 us
    ppermute x4, waiting for transfers between devices, shifted(): return lax.ppermute(block, axis, route)  4 us
  transfers between devices with their start and end apart: 6, of which 4 were waited for; matrix products, arithmetic and copies ran while one was open for 18% of the time, Pallas kernels for 0%

commit v1 on v0

v1 whole, which is shorter than its diff:
```python
import functools

import jax
import jax.numpy as jnp
from jax import lax
from jax.experimental import pallas as pl
from jax.experimental.pallas import tpu as pltpu
from jax.sharding import PartitionSpec as P


HEADS = 128
attn_scale = 192.0 ** (-0.5)
F32 = jnp.float32
BF16 = jnp.bfloat16


def each(count, step):
    if count <= 2:
        for i in range(count):
            step(i)
    else:
        lax.fori_loop(0, count, lambda i, _: (step(i), None)[1], None)


def vmem():
    return pl.BlockSpec(memory_space=pltpu.VMEM)


def smem():
    return pl.BlockSpec(memory_space=pltpu.SMEM)


def call(kernel, out_shape, in_specs, scratch=(), limit=8 << 20, flops=0, moved=0):
    return pl.pallas_call(
        kernel,
        out_shape=out_shape,
        in_specs=in_specs,
        out_specs=jax.tree.map(lambda _: vmem(), out_shape),
        scratch_shapes=list(scratch),
        cost_estimate=pl.CostEstimate(flops=flops, bytes_accessed=moved, transcendentals=0),
        compiler_params=pltpu.CompilerParams(vmem_limit_bytes=limit),
    )


def block_sums(query, keys_ref, lse_ref, iquery_ref, ikey_ref, weight_ref, part_ref, active_ref, pair_ref):
    index_width = ikey_ref.shape[1]
    iheads = iquery_ref.shape[1] // index_width
    keys, tokens = part_ref.shape[1:]
    index_scale = index_width ** (-0.5)
    score = jnp.zeros((keys, tokens), F32)
    for j in range(iheads):
        logits = lax.dot_general(
            ikey_ref[...],
            iquery_ref[:, j * index_width : (j + 1) * index_width],
            (((1,), (1,)), ((), ())),
            preferred_element_type=F32,
        )
        active = jnp.maximum(logits * index_scale, 0.0)
        active_ref[:, j * tokens : (j + 1) * tokens] = active
        score = score + active * weight_ref[j : j + 1, :]
    part_ref[1] = score

    width = keys_ref.shape[0]
    pair_ref[...] = jnp.zeros_like(pair_ref)
    pair_ref[:width, :keys] = keys_ref[...]
    pair_ref[width:, keys:] = keys_ref[...]
    lse_columns = jnp.transpose(lse_ref[...])
    total = jnp.zeros((tokens, keys), F32)
    for p in range(lse_ref.shape[0] // 2):
        both = jnp.dot(query(p), pair_ref[...], preferred_element_type=F32)
        for side in range(2):
            h = 2 * p + side
            scores = both[:, side * keys : (side + 1) * keys] * attn_scale
            total = total + jnp.exp(scores - lse_columns[:, h : h + 1])
    part_ref[0] = jnp.transpose(total) * (1.0 / HEADS)


def own_kernel(
    query_hbm, keys_hbm, lse_hbm, iquery_hbm, ikey_hbm, weight_hbm,
    part_ref, active_ref, query_ref, lse_ref, iquery_ref, ikey_ref, weight_ref,
    pair_ref, keys_ref, sems,
):
    width = keys_ref.shape[0]
    pairs = query_ref.shape[1] // (2 * width)
    moves = [
        pltpu.make_async_copy(src, dst, sems.at[i])
        for i, (src, dst) in enumerate(
            (
                (ikey_hbm, ikey_ref),
                (iquery_hbm, iquery_ref),
                (weight_hbm, weight_ref),
                (lse_hbm, lse_ref),
                (keys_hbm, keys_ref),
            )
        )
    ]
    chunks = sems.shape[0] - len(moves)
    span = pairs // chunks * 2 * width
    moves += [
        pltpu.make_async_copy(
            query_hbm.at[:, i * span : (i + 1) * span],
            query_ref.at[:, i * span : (i + 1) * span],
            sems.at[len(moves) + i],
        )
        for i in range(chunks)
    ]
    for move in moves:
        move.start()
    for move in moves[:5]:
        move.wait()

    def query(p):
        if p % (pairs // chunks) == 0:
            moves[5 + p // (pairs // chunks)].wait()
        return query_ref[:, 2 * p * width : 2 * (p + 1) * width]

    block_sums(
        query, keys_ref, lse_ref, iquery_ref, ikey_ref, weight_ref, part_ref, active_ref, pair_ref
    )


def other_kernel(query_ref, keys_ref, lse_ref, iquery_ref, ikey_ref, weight_ref, part_ref, active_ref, pair_ref):
    width = keys_ref.shape[0]

    def query(p):
        return query_ref[:, 2 * p * width : 2 * (p + 1) * width]

    block_sums(
        query, keys_ref, lse_ref, iquery_ref, ikey_ref, weight_ref, part_ref, active_ref, pair_ref
    )


def key_grad_kernel(
    blocks, order_ref, chip_ref, recv_ref, lse_ref, active_ref, weight_ref, iquery_ref,
    grad_ref, coef_ref, diff_ref,
):
    keys, tokens = chip_ref.shape[2:]
    index_width = grad_ref.shape[2]
    iheads = weight_ref.shape[0]
    index_scale = index_width ** (-0.5)
    place = lax.axis_index("wide")

    def block(b):
        source = lax.rem(place - b + blocks, blocks)
        target = chip_ref[b, 0] + recv_ref[b, 0].astype(F32)
        score = chip_ref[b, 1] + recv_ref[b, 1].astype(F32)
        key_at = lax.broadcasted_iota(jnp.int32, (keys, tokens), 0)
        query_at = lax.broadcasted_iota(jnp.int32, (keys, tokens), 1)
        causal = (order_ref[place] - order_ref[source]) * tokens + query_at >= key_at
        difference = jnp.where(causal, jnp.exp(score - lse_ref[...]) - target, 0.0)
        diff_ref[b] = difference
        for j in range(iheads):
            scaled = difference * (weight_ref[j : j + 1, :] * index_scale)
            coef = jnp.where(active_ref[b, :, j * tokens : (j + 1) * tokens] > 0.0, scaled, 0.0)
            coef_ref[b, :, j * tokens : (j + 1) * tokens] = coef.astype(BF16)
        total = jnp.zeros((keys, index_width), F32)
        for p in range(iheads // 2):
            rows = jnp.concatenate(
                [
                    iquery_ref[:, (2 * p + i) * index_width : (2 * p + i + 1) * index_width]
                    for i in range(2)
                ],
                axis=0,
            )
            total = total + jnp.dot(
                coef_ref[b, :, 2 * p * tokens : 2 * (p + 1) * tokens],
                rows,
                preferred_element_type=F32,
            )
        grad_ref[b] = total

    each(blocks, block)


def query_grad_kernel(blocks, coef_ref, diff_ref, active_ref, ikey_ref, grad_ref, weight_grad_ref):
    _, tokens = diff_ref.shape[1:]
    index_width = ikey_ref.shape[2]
    iheads = weight_grad_ref.shape[0]
    grad_ref[...] = jnp.zeros_like(grad_ref)
    weight_grad_ref[...] = jnp.zeros_like(weight_grad_ref)

    def block(b):
        for j in range(iheads):
            at = slice(j * tokens, (j + 1) * tokens)
            grad_ref[:, j * index_width : (j + 1) * index_width] += lax.dot_general(
                coef_ref[b, :, at], ikey_ref[b], (((0,), (0,)), ((), ())), preferred_element_type=F32
            )
            weight_grad_ref[j : j + 1, :] += jnp.sum(
                diff_ref[b] * active_ref[b, :, at], axis=0, keepdims=True
            )

    each(blocks, block)


def body(
    attn_query, key_latent, lse_attn, index_query, index_key, index_weight, lse_index, block_order
):
    tokens, key_width = key_latent.shape
    index_width = index_key.shape[1]
    heads = attn_query.shape[1] // key_width
    iheads = index_query.shape[1] // index_width
    wide, narrow = lax.axis_size("wide"), lax.axis_size("narrow")
    ranks = range(wide * narrow)

    def send(block, step, flip):
        route = [(r, (r // narrow - step) % wide * narrow + (r % narrow ^ flip)) for r in ranks]
        return lax.ppermute(block, ("wide", "narrow"), route)

    own_keys = jnp.transpose(key_latent)
    keys, ikeys = [own_keys], [index_key]
    for b in range(1, wide):
        keys.append(send(own_keys, -b, 0))
        ikeys.append(send(index_key, -b, 0))

    like = jax.ShapeDtypeStruct
    part = like((2, tokens, tokens), F32)
    act = like((tokens, iheads * tokens), F32)
    pair_shape = pltpu.VMEM((2 * key_width, 2 * tokens), BF16)
    work = dict(
        flops=2 * tokens * tokens * (heads * key_width + iheads * index_width),
        moved=attn_query.size * 2,
    )
    inputs = (attn_query, own_keys, lse_attn, index_query, index_key, index_weight)
    chunks = 4 if heads % 8 == 0 else 1
    own = call(
        own_kernel,
        (part, act)
        + tuple(like(a.shape, a.dtype) for a in (attn_query, lse_attn, index_query, index_key, index_weight)),
        [pl.BlockSpec(memory_space=pltpu.MemorySpace.HBM)] * 6,
        [pair_shape, pltpu.VMEM(own_keys.shape, BF16), pltpu.SemaphoreType.DMA((5 + chunks,))],
        limit=14 << 20,
        **work,
    )(*(pltpu.with_memory_space_constraint(x, pltpu.MemorySpace.HBM) for x in inputs))
    query, lse, iquery, ikey, weight = own[2:]
    other = call(other_kernel, (part, act), [vmem()] * 6, [pair_shape], limit=14 << 20, **work)
    found = [own[:2]] + [
        other(query, k, lse, iquery, ik, weight) for k, ik in zip(keys[1:], ikeys[1:])
    ]
    ikeys[0] = ikey
    active = jnp.stack([a for _, a in found])
    chip = jnp.stack([p + send(p, 0, 1) for p, _ in found])
    recv = send(chip.astype(BF16), 0, 2)

    grad, coef, difference = call(
        functools.partial(key_grad_kernel, wide),
        (
            jax.ShapeDtypeStruct((wide, tokens, index_width), F32),
            jax.ShapeDtypeStruct((wide, tokens, iheads * tokens), BF16),
            jax.ShapeDtypeStruct((wide, tokens, tokens), F32),
        ),
        [smem()] + [vmem()] * 6,
        limit=16 << 20,
        flops=2 * wide * tokens * tokens * iheads * index_width,
        moved=wide * tokens * tokens * iheads * 6,
    )(block_order, chip, recv, lse_index[None, :], active, weight, iquery)

    grad_query, grad_weight = call(
        functools.partial(query_grad_kernel, wide),
        (
            jax.ShapeDtypeStruct((tokens, iheads * index_width), F32),
            jax.ShapeDtypeStruct((iheads, tokens), F32),
        ),
        [vmem()] * 4,
        limit=16 << 20,
        flops=2 * wide * tokens * tokens * iheads * index_width,
        moved=wide * tokens * tokens * iheads * 6,
    )(coef, difference, active, jnp.stack(ikeys))

    pair = (grad + send(grad, 0, 1)).astype(BF16)
    key_grad = jnp.zeros((tokens, index_width), F32)
    for b in range(wide):
        near = send(pair[b], b, 0) if b else pair[b]
        far = send(pair[b], b, 2)
        key_grad = key_grad + (near.astype(F32) + far.astype(F32))
    return grad_query, grad_weight, key_grad


def solution(mesh):
    in_specs = (
        P(("seq", "wide"), "narrow"),
        P(("seq", "wide"), None),
        P("narrow", ("seq", "wide")),
        P(("seq", "wide"), "narrow"),
        P(("seq", "wide"), None),
        P("narrow", ("seq", "wide")),
        P(("seq", "wide")),
        P("seq"),
    )
    out_specs = (
        P(("seq", "wide"), "narrow"),
        P("narrow", ("seq", "wide")),
        P(("seq", "wide"), None),
    )
    return jax.shard_map(
        body,
        mesh=mesh,
        in_specs=in_specs,
        out_specs=out_specs,
        check_vma=False,
    )
```

time: 120 us -> 31.7 us (0.26)
  waiting for transfers between devices: 67.9 us -> 12.3 us
  between operations: 16.2 us -> 0.75 us
  matrix products: 13.6 us -> 0 us
  local copies, waits for them, and re-layouts: 12.4 us -> 0.02 us
  Pallas kernels: 0 us -> 9.09 us
  other arithmetic: 3.2 us -> 0.9 us
  starting transfers between devices: 6.27 us -> 8.42 us
    psum x2 -> x0, waiting for transfers between devices: 63.9 us -> none  [the longest x1 34.1 us: block_grads(): target, score = lax.psum((part_target, part_score), 'narrow')]
    dot_general x12 -> x0, matrix products: 13.6 us -> none  [the longest x2 6.66 us: block_grads(): jnp.einsum('thc,sc->ths', query_heads, key_block, preferred_element_type=...]
    unnamed x21 -> x6, local copies, waits for them, and re-layouts: 10.1 us -> 0.01 us
    pallas_call x0 -> x4, Pallas kernels: none -> 9.09 us  [the longest x1 4.13 us: body(): call(own_kernel, (part, act) + tuple((like(a.shape, a.dtype) for a in (at...]
    ppermute x4 -> x9, waiting for transfers between devices: 4 us -> 12.3 us  [send(): return lax.ppermute(block, ('wide', 'narrow'), route)]
    ppermute x4 -> x9, starting transfers between devices: 6.19 us -> 8.42 us  [send(): return lax.ppermute(block, ('wide', 'narrow'), route)]
    dynamic_slice x1 -> x0, local copies, waits for them, and re-layouts: 1.36 us -> none  [block_grads(): key_pos = block_order[source] * tok_rows + offsets]
    div x2 -> x0, other arithmetic: 1.27 us -> none  [block_grads(): jnp.sum(jnp.exp(scores - lse_rows[:, :, None]), axis=1) / HEADS]
  transfers between devices with their start and end apart: 6 -> 9, of which waited for: 4 -> 5; matrix products, arithmetic and copies ran while one was open for 18% -> 1% of each run, Pallas kernels for 0% -> 25%
where the time goes in v1:
time: 31.7 us; the launch traced here: 31.5 us
  waiting for transfers between devices  12.3 us (39%)
  Pallas kernels  9.09 us (29%)
  starting transfers between devices  8.42 us (27%)
  other arithmetic  0.9 us (3%)
  between operations  0.75 us (2%)
    ppermute x9, waiting for transfers between devices, send(): return lax.ppermute(block, ('wide', 'narrow'), route)  12.3 us
    ppermute x9, starting transfers between devices, send(): return lax.ppermute(block, ('wide', 'narrow'), route)  8.42 us
    pallas_call x1, Pallas kernels, body(): call(own_kernel, (part, act) + tuple((like(a.shape, a.dtype) for a in (at...  4.13 us
    pallas_call x1, Pallas kernels, body(): other(query, k, lse, iquery, ik, weight)  2.2 us
    pallas_call x1, Pallas kernels, body(): call(functools.partial(query_grad_kernel, wide), (jax.ShapeDtypeStruct((t...  1.45 us
    pallas_call x1, Pallas kernels, body(): call(functools.partial(key_grad_kernel, wide), (jax.ShapeDtypeStruct((wid...  1.32 us
    add x1, other arithmetic, body(): key_grad = key_grad + (near.astype(F32) + far.astype(F32))  0.65 us
  transfers between devices with their start and end apart: 9, of which 5 were waited for; matrix products, arithmetic and copies ran while one was open for 1% of the time, Pallas kernels for 25%

profile of v1, /device:TPU:0, one launch (start us, length us, event | category | flops | bytes accessed | tf_op | source)
XLA Modules:
  0.0 31.5 jit_solution(7228352319566063386)
XLA Ops:
  0.6 0.0 copy-start.2
  0.6 3.0 %collective-permute-start.1 = (bf16[576,128]{1,0:T(8,128)(2,1)}, bf16[576,128]{1,0:T(8,128)(2,1)S(1)}, u32[]{:S(2)}, u32[]{:S(2)}) collective-permute-start(bf16[576,128]{1,0:T(8,128)(2,1)} %bitcast.21), channel_id=1, source_target_pairs={{0,16},{4,20},{8,24},{12,28},{16,0},{20,4},{24,8},{28,12},{1,17},{... | collective-permute-start | bytes 442376 | tf_op jit(solution)/shard_map/ppermute | solution.py:207
  3.7 4.1 %shard_map.103 = (f32[2,128,128]{2,1,0:T(8,128)S(1)}, f32[128,2048]{1,0:T(8,128)S(1)}, bf16[128,18432]{1,0:T(8,128)(2,1)S(1)}, f32[32,128]{1,0:T(8,128)S(1)}, bf...) custom-call(bf16[128,18432]{1,0:T(8,128)(2,1)} %query_hbm.1, ...), custom_call_target="tpu_custom_call" | custom-call | flops 671088640 | bytes 4718592 | tf_op jit(solution)/shard_map/pallas_call | solution.py:225
  7.8 0.1 collective-permute-start
  7.9 0.0 copy-done.2
  7.9 0.1 collective-permute-start.2
  8.0 3.9 %collective-permute-done.2.ikey_ref = bf16[128,128]{1,0:T(8,128)(2,1)S(1)} collective-permute-done((bf16[128,128]{1,0:T(8,128)(2,1)S(1)}, bf16[128,128]{1,0:T(8,128)(2,1)S(1)}, u32[]{:S(2)}, u32[]{:S(2)}) %collective-permute-start.2) | collective-permute-done | bytes 32800 | tf_op jit(solution)/shard_map/ppermute | solution.py:207
  11.9 0.0 collective-permute-done.1.keys_ref
  11.9 2.2 %shard_map.104 = (f32[2,128,128]{2,1,0:T(8,128)S(1)}, f32[128,2048]{1,0:T(8,128)S(1)}) custom-call(bf16[128,18432]{1,0:T(8,128)(2,1)S(1)} %get-tuple-element.18.query_ref, bf16[576,128]{1,0:T(8,128)(2,1)S(1)} %collective-permute-done.1.keys_ref, f32[32,128]{1,0:T(8,128)S(1)} %get-tuple-element.19.lse_ref, ...), custom_call_target="tpu_custom_call" | custom-call | flops 671088640 | bytes 4718592 | tf_op jit(solution)/shard_map/pallas_call | solution.py:237
  14.1 0.1 collective-permute-start.3
  14.2 0.0 collective-permute-done
  14.2 1.3 %collective-permute-done.3 = f32[2,128,128]{2,1,0:T(8,128)S(1)} collective-permute-done((f32[2,128,128]{2,1,0:T(8,128)S(1)}, f32[2,128,128]{2,1,0:T(8,128)S(1)}, u32[]{:S(2)}, u32[]{:S(2)}) %collective-permute-start.3) | collective-permute-done | bytes 131104 | tf_op jit(solution)/shard_map/ppermute | solution.py:207
  15.6 1.6 %collective-permute-start.4 = (bf16[2,2,128,128]{3,2,1,0:T(8,128)(2,1)S(1)}, bf16[2,2,128,128]{3,2,1,0:T(8,128)(2,1)S(1)}, u32[]{:S(2)}, u32[]{:S(2)}) collective-permute-start(bf16[2,2,128,128]{3,2,1,0:T(8,128)(2,1)S(1)} %fusion), channel_id=1, source_target_pairs={{0,8},{4,12},{8,0},{12,4},{16,24},{20,28},{24,16},{28,20},{1,9},{5... | collective-permute-start | bytes 393224 | tf_op jit(solution)/shard_map/ppermute | solution.py:207
  17.1 0.0 copy-start
  17.1 0.0 copy-start.1
  17.1 0.1 pad_maximum_fusion.active_ref
  17.3 3.9 %collective-permute-done.4.recv_ref = bf16[2,2,128,128]{3,2,1,0:T(8,128)(2,1)S(1)} collective-permute-done((bf16[2,2,128,128]{3,2,1,0:T(8,128)(2,1)S(1)}, bf16[2,2,128,128]{3,2,1,0:T(8,128)(2,1)S(1)}, u32[]{:S(2)}, u32[]{:S(2)}) %collective-permute-start.4) | collective-permute-done | bytes 131104 | tf_op jit(solution)/shard_map/ppermute | solution.py:207
  21.2 0.0 copy-done
  21.2 0.0 copy-done.1
  21.2 1.3 %shard_map.105 = (f32[2,128,128]{2,1,0:T(8,128)S(1)}, bf16[2,128,2048]{2,1,0:T(8,128)(2,1)S(1)}, f32[2,128,128]{2,1,0:T(8,128)S(1)}) custom-call(s32[2]{0:T(128)S(1)} %copy-done, f32[2,2,128,128]{3,2,1,0:T(8,128)S(1)} %pad_maximum_fusion.1.chip_ref, bf16[2,2,128,128]{3,2,1,0:T(8,128)(2,1)S(1)} %collective-permute-done.4.recv_ref, f32[1,128]{1,0:T(1,128)S(1)} %bitcast.20, ...), custom_call_target="tpu_custom_call" | custom-call | flops 134217728 | bytes 3145728 | tf_op jit(solution)/shard_map/pallas_call | solution.py:244
  22.5 0.1 collective-permute-start.5
  22.6 1.3 %collective-permute-done.5 = f32[2,128,128]{2,1,0:T(8,128)S(1)} collective-permute-done((f32[2,128,128]{2,1,0:T(8,128)S(1)}, f32[2,128,128]{2,1,0:T(8,128)S(1)}, u32[]{:S(2)}, u32[]{:S(2)}) %collective-permute-start.5) | collective-permute-done | bytes 131104 | tf_op jit(solution)/shard_map/ppermute | solution.py:207
  23.9 1.5 %collective-permute-start.8 = (bf16[128,128]{1,0:T(8,128)(2,1)S(1)}, bf16[128,128]{1,0:T(8,128)(2,1)S(1)}, u32[]{:S(2)}, u32[]{:S(2)}) collective-permute-start(bf16[128,128]{1,0:T(8,128)(2,1)S(1)} %get-tuple-element.32), channel_id=1, source_target_pairs={{0,24},{4,28},{8,16},{12,20},{16,8},{20,12},{24,0},{28,4},{1,25},{... | collective-permute-start | bytes 98312 | tf_op jit(solution)/shard_map/ppermute | solution.py:207
  25.5 1.5 %collective-permute-start.7 = (bf16[128,128]{1,0:T(8,128)(2,1)S(1)}, bf16[128,128]{1,0:T(8,128)(2,1)S(1)}, u32[]{:S(2)}, u32[]{:S(2)}) collective-permute-start(bf16[128,128]{1,0:T(8,128)(2,1)S(1)} %get-tuple-element.32), channel_id=1, source_target_pairs={{0,16},{4,20},{8,24},{12,28},{16,0},{20,4},{24,8},{28,12},{1,17},{... | collective-permute-start | bytes 98312 | tf_op jit(solution)/shard_map/ppermute | solution.py:207
  27.0 0.5 %collective-permute-start.6 = (bf16[128,128]{1,0:T(8,128)(2,1)S(1)}, bf16[128,128]{1,0:T(8,128)(2,1)S(1)}, u32[]{:S(2)}, u32[]{:S(2)}) collective-permute-start(bf16[128,128]{1,0:T(8,128)(2,1)S(1)} %get-tuple-element.31), channel_id=1, source_target_pairs={{0,8},{4,12},{8,0},{12,4},{16,24},{20,28},{24,16},{28,20},{1,9},{5... | collective-permute-start | bytes 98312 | tf_op jit(solution)/shard_map/ppermute | solution.py:207
  27.5 1.4 %shard_map.106 = (f32[128,2048]{1,0:T(8,128)}, f32[16,128]{1,0:T(8,128)}) custom-call(bf16[2,128,2048]{2,1,0:T(8,128)(2,1)S(1)} %get-tuple-element.25.coef_ref, f32[2,128,128]{2,1,0:T(8,128)S(1)} %get-tuple-element.26.diff_ref, f32[2,128,2048]{2,1,0:T(8,128)S(1)} %pad_maximum_fusion.active_ref, bf16[2,128,128]{2,1,0:T(8,128)(2,1)S(1)} %pad_maximum_fusion.2.ikey_ref), custom_call_target="tpu_custom_call" | custom-call | flops 134217728 | bytes 3145728 | tf_op jit(solution)/shard_map/pallas_call | solution.py:257
  29.0 1.9 %collective-permute-done.6 = bf16[128,128]{1,0:T(8,128)(2,1)S(1)} collective-permute-done((bf16[128,128]{1,0:T(8,128)(2,1)S(1)}, bf16[128,128]{1,0:T(8,128)(2,1)S(1)}, u32[]{:S(2)}, u32[]{:S(2)}) %collective-permute-start.6) | collective-permute-done | bytes 32800 | tf_op jit(solution)/shard_map/ppermute | solution.py:207
  30.9 0.0 collective-permute-done.8
  30.9 0.0 collective-permute-done.7
  30.9 0.6 %add_add_fusion = f32[128,128]{1,0:T(8,128)} fusion(bf16[128,128]{1,0:T(8,128)(2,1)S(1)} %collective-permute-done.8, bf16[128,128]{1,0:T(8,128)(2,1)S(1)} %collective-permute-done.7, bf16[128,128]{1,0:T(8,128)(2,1)S(1)} %collective-permute-done.6, bf16[2,128,128]{2,1,0:T(8,128)(2,1)S(1)} %add_convert_fusion), kind=kLoop, calls=%fused_computation.6 | loop fusion | flops 114688 | bytes 196608 | tf_op jit(solution)/shard_map/add | solution.py:274
  (7 shorter events, 0.1 us)
Async XLA Ops:
  0.6 7.3 %copy-start.2 = (bf16[128,128]{1,0:T(8,128)(2,1)S(1)}, bf16[128,128]{1,0:T(8,128)(2,1)}, u32[]{:S(2)}) copy-start(bf16[128,128]{1,0:T(8,128)(2,1)} %ikey_hbm.1) | copy-start | bytes 98308
  0.6 11.2 %collective-permute-start.1 = (bf16[576,128]{1,0:T(8,128)(2,1)}, bf16[576,128]{1,0:T(8,128)(2,1)S(1)}, u32[]{:S(2)}, u32[]{:S(2)}) collective-permute-start(bf16[576,128]{1,0:T(8,128)(2,1)} %bitcast.21), channel_id=1, source_target_pairs={{0,16},{4,20},{8,24},{12,28},{16,0},{20,4},{24,8},{28,12},{1,17},{... | collective-permute-start | bytes 442376 | tf_op jit(solution)/shard_map/ppermute | solution.py:207
  7.8 6.4 %collective-permute-start = (f32[2,128,128]{2,1,0:T(8,128)S(1)}, f32[2,128,128]{2,1,0:T(8,128)S(1)}, u32[]{:S(2)}, u32[]{:S(2)}) collective-permute-start(f32[2,128,128]{2,1,0:T(8,128)S(1)} %get-tuple-element.17), channel_id=1, source_target_pairs={{0,4},{4,0},{8,12},{12,8},{16,20},{20,16},{24,28},{28,24},{1,5},{5... | collective-permute-start | bytes 393224 | tf_op jit(solution)/shard_map/ppermute | solution.py:207
  7.9 4.0 %collective-permute-start.2 = (bf16[128,128]{1,0:T(8,128)(2,1)S(1)}, bf16[128,128]{1,0:T(8,128)(2,1)S(1)}, u32[]{:S(2)}, u32[]{:S(2)}) collective-permute-start(bf16[128,128]{1,0:T(8,128)(2,1)S(1)} %copy-done.2), channel_id=1, source_target_pairs={{0,16},{4,20},{8,24},{12,28},{16,0},{20,4},{24,8},{28,12},{1,17},{... | collective-permute-start | bytes 98312 | tf_op jit(solution)/shard_map/ppermute | solution.py:207
  14.1 1.4 %collective-permute-start.3 = (f32[2,128,128]{2,1,0:T(8,128)S(1)}, f32[2,128,128]{2,1,0:T(8,128)S(1)}, u32[]{:S(2)}, u32[]{:S(2)}) collective-permute-start(f32[2,128,128]{2,1,0:T(8,128)S(1)} %get-tuple-element.22), channel_id=1, source_target_pairs={{0,4},{4,0},{8,12},{12,8},{16,20},{20,16},{24,28},{28,24},{1,5},{5... | collective-permute-start | bytes 393224 | tf_op jit(solution)/shard_map/ppermute | solution.py:207
  15.6 5.6 %collective-permute-start.4 = (bf16[2,2,128,128]{3,2,1,0:T(8,128)(2,1)S(1)}, bf16[2,2,128,128]{3,2,1,0:T(8,128)(2,1)S(1)}, u32[]{:S(2)}, u32[]{:S(2)}) collective-permute-start(bf16[2,2,128,128]{3,2,1,0:T(8,128)(2,1)S(1)} %fusion), channel_id=1, source_target_pairs={{0,8},{4,12},{8,0},{12,4},{16,24},{20,28},{24,16},{28,20},{1,9},{5... | collective-permute-start | bytes 393224 | tf_op jit(solution)/shard_map/ppermute | solution.py:207
  17.1 4.1 %copy-start = (s32[2]{0:T(128)S(1)}, s32[2]{0:T(128)}, u32[]{:S(2)}) copy-start(s32[2]{0:T(128)} %order_ref.1) | copy-start | bytes 28
  17.1 4.1 %copy-start.1 = (f32[128]{0:T(128)S(1)}, f32[128]{0:T(128)}, u32[]{:S(2)}) copy-start(f32[128]{0:T(128)} %param.14) | copy-start | bytes 1540
  22.5 1.4 %collective-permute-start.5 = (f32[2,128,128]{2,1,0:T(8,128)S(1)}, f32[2,128,128]{2,1,0:T(8,128)S(1)}, u32[]{:S(2)}, u32[]{:S(2)}) collective-permute-start(f32[2,128,128]{2,1,0:T(8,128)S(1)} %get-tuple-element.30), channel_id=1, source_target_pairs={{0,4},{4,0},{8,12},{12,8},{16,20},{20,16},{24,28},{28,24},{1,5},{5... | collective-permute-start | bytes 393224 | tf_op jit(solution)/shard_map/ppermute | solution.py:207
  23.9 6.9 %collective-permute-start.8 = (bf16[128,128]{1,0:T(8,128)(2,1)S(1)}, bf16[128,128]{1,0:T(8,128)(2,1)S(1)}, u32[]{:S(2)}, u32[]{:S(2)}) collective-permute-start(bf16[128,128]{1,0:T(8,128)(2,1)S(1)} %get-tuple-element.32), channel_id=1, source_target_pairs={{0,24},{4,28},{8,16},{12,20},{16,8},{20,12},{24,0},{28,4},{1,25},{... | collective-permute-start | bytes 98312 | tf_op jit(solution)/shard_map/ppermute | solution.py:207
  25.5 5.4 %collective-permute-start.7 = (bf16[128,128]{1,0:T(8,128)(2,1)S(1)}, bf16[128,128]{1,0:T(8,128)(2,1)S(1)}, u32[]{:S(2)}, u32[]{:S(2)}) collective-permute-start(bf16[128,128]{1,0:T(8,128)(2,1)S(1)} %get-tuple-element.32), channel_id=1, source_target_pairs={{0,16},{4,20},{8,24},{12,28},{16,0},{20,4},{24,8},{28,12},{1,17},{... | collective-permute-start | bytes 98312 | tf_op jit(solution)/shard_map/ppermute | solution.py:207
  27.0 3.9 %collective-permute-start.6 = (bf16[128,128]{1,0:T(8,128)(2,1)S(1)}, bf16[128,128]{1,0:T(8,128)(2,1)S(1)}, u32[]{:S(2)}, u32[]{:S(2)}) collective-permute-start(bf16[128,128]{1,0:T(8,128)(2,1)S(1)} %get-tuple-element.31), channel_id=1, source_target_pairs={{0,8},{4,12},{8,0},{12,4},{16,24},{20,28},{24,16},{28,20},{1,9},{5... | collective-permute-start | bytes 98312 | tf_op jit(solution)/shard_map/ppermute | solution.py:207

commit v2 on v0

v2 whole, which is shorter than its diff:
```python
import functools
import math

import jax
import jax.numpy as jnp
from jax import lax
from jax.experimental import pallas as pl
from jax.experimental.pallas import tpu as pltpu
from jax.sharding import PartitionSpec as P


HEADS = 128
SPAN = 8
CHUNKS = 2
attn_scale = 192.0 ** (-0.5)
F32 = jnp.float32
BF16 = jnp.bfloat16


def vmem():
    return pl.BlockSpec(memory_space=pltpu.VMEM)


def call(kernel, out_shape, in_specs, scratch=(), limit=8 << 20, flops=0, moved=0):
    return pl.pallas_call(
        kernel,
        out_shape=out_shape,
        in_specs=in_specs,
        out_specs=jax.tree.map(lambda _: vmem(), out_shape),
        scratch_shapes=list(scratch),
        cost_estimate=pl.CostEstimate(flops=flops, bytes_accessed=moved, transcendentals=0),
        compiler_params=pltpu.CompilerParams(vmem_limit_bytes=limit),
    )


def side_by_side(refs):
    return jnp.concatenate([ref[...] for ref in refs], axis=1)


def block_sums(turned, packed, lse_ref, iturned_ref, weight_ref, part_ref, active_ref):
    tokens = part_ref.shape[2]
    heads, iheads = lse_ref.shape[0], weight_ref.shape[0]
    index_width = iturned_ref.shape[0] // iheads
    index_scale = index_width ** (-0.5)
    width = packed.shape[0] - index_width
    late = -width % 128
    fill = jnp.zeros((late, packed.shape[1]), BF16)
    sides = [
        jnp.transpose(jnp.concatenate(parts, axis=0)) if late else jnp.transpose(packed[:width])
        for parts in ((packed[:width], fill), (fill, packed[:width]))
    ]
    score = 0.0
    for j in range(0, iheads, 2):
        rows = [iturned_ref.at[i * index_width : (i + 1) * index_width] for i in (j, j + 1)]
        logits = jnp.dot(packed[width:], side_by_side(rows), preferred_element_type=F32)
        active = jnp.maximum(logits * index_scale, 0.0)
        active_ref[:, j * tokens : (j + 2) * tokens] = active
        for i in range(2):
            score = score + active[:, i * tokens : (i + 1) * tokens] * weight_ref[j + i : j + i + 1, :]
    part_ref[1] = score

    total = 0.0
    for p in range(0, heads // 2, 2):
        pairs = [turned(p), turned(p + 1)]
        for side, keys in enumerate(sides):
            first = side * (width - late)
            rows = [pair.at[first : first + width + late] for pair in pairs]
            both = jnp.dot(keys, side_by_side(rows), preferred_element_type=F32) * attn_scale
            for i in range(2):
                h = 2 * (p + i) + side
                total = total + jnp.exp(both[:, i * tokens : (i + 1) * tokens] - lse_ref[h : h + 1, :])
    part_ref[0] = total * (1.0 / HEADS)


def load_kernel(order_hbm, *refs):
    count = (len(refs) - 3) // 2
    sources, held = refs[:count], refs[count : 2 * count - 1]
    mine_ref, live_ref, order_ref, sems = refs[2 * count - 1 :]
    packed_ref = held[0]
    width = sources[0].shape[0]
    held = (packed_ref.at[:width], packed_ref.at[width:], *held[1:])
    moves = [
        pltpu.make_async_copy(src, dst, sems.at[i])
        for i, (src, dst) in enumerate(zip((order_hbm, *sources), (order_ref, *held)))
    ]
    for move in moves:
        move.start()
    for move in moves:
        move.wait()
    half = mine_ref.shape[0]
    core = lax.axis_index("narrow") % 2
    mine_ref[...] = packed_ref[pl.ds(pl.multiple_of(core * half, half), half)]

    place, blocks = lax.axis_index("wide"), live_ref.shape[0]
    for b in range(blocks):
        source = lax.rem(place - b + blocks, blocks)
        live = (order_ref[place] > order_ref[source]).astype(F32)
        live_ref[b] = jnp.full(live_ref.shape[1:], live, F32)


def own_kernel(
    query_hbm, packed_ref, iquery_ref, lse_ref, weight_ref,
    part_ref, active_ref, turned_ref, iturned_ref, query_ref, sems,
):
    pair_width = query_ref.shape[1] // lse_ref.shape[0] * 2
    step = query_ref.shape[1] // sems.shape[0]
    moves = []
    for i in range(sems.shape[0]):
        at = slice(i * step, (i + 1) * step)
        moves.append(pltpu.make_async_copy(query_hbm.at[:, at], query_ref.at[:, at], sems.at[i]))
        moves[-1].start()

    def turned(p):
        at = p * pair_width
        if at % step == 0:
            moves[at // step].wait()
        at = slice(at, at + pair_width)
        turned_ref[at] = jnp.transpose(query_ref[:, at])
        return turned_ref.at[at]

    @pl.when(lax.axis_index("wide") >= 0)
    def _():
        index_width = iquery_ref.shape[1] // weight_ref.shape[0]
        for j in range(weight_ref.shape[0]):
            at = slice(j * index_width, (j + 1) * index_width)
            iturned_ref[at] = jnp.transpose(iquery_ref[:, at])
        block_sums(turned, packed_ref, lse_ref, iturned_ref, weight_ref, part_ref, active_ref)


def other_kernel(
    turned_ref, mine_ref, theirs_ref, lse_ref, iturned_ref, weight_ref,
    part_ref, active_ref, ikey_ref, packed_ref,
):
    pair_width = turned_ref.shape[0] // lse_ref.shape[0] * 2
    half = mine_ref.shape[0]
    core = lax.axis_index("narrow") % 2
    packed_ref[pl.ds(pl.multiple_of(core * half, half), half)] = mine_ref[...]
    packed_ref[pl.ds(pl.multiple_of((1 - core) * half, half), half)] = theirs_ref[...]
    ikey_ref[...] = packed_ref[packed_ref.shape[0] - ikey_ref.shape[0] :]

    def turned(p):
        return turned_ref.at[p * pair_width : (p + 1) * pair_width]

    block_sums(turned, packed_ref, lse_ref, iturned_ref, weight_ref, part_ref, active_ref)


def key_grad_kernel(
    step, live_ref, mine_ref, theirs_ref, lse_ref, active_ref, weight_ref, iquery_ref,
    grad_ref, coef_ref, diff_ref,
):
    keys, tokens = mine_ref.shape[1:]
    index_width = grad_ref.shape[1]
    iheads = weight_ref.shape[0]
    index_scale = index_width ** (-0.5)
    target = mine_ref[0] + theirs_ref[0]
    score = mine_ref[1] + theirs_ref[1]
    if step == 0:
        key_at = lax.broadcasted_iota(jnp.int32, (keys, tokens), 0)
        query_at = lax.broadcasted_iota(jnp.int32, (keys, tokens), 1)
        causal = query_at >= key_at
    else:
        causal = jnp.broadcast_to(live_ref[step], (keys, tokens)) > 0.0
    difference = jnp.where(causal, jnp.exp(score - lse_ref[...]) - target, 0.0)
    diff_ref[...] = difference
    total = jnp.zeros((keys, index_width), F32)
    span = math.gcd(iheads, SPAN)
    for first in range(0, iheads, span):
        for j in range(first, first + span):
            scaled = difference * (weight_ref[j : j + 1, :] * index_scale)
            coef = jnp.where(active_ref[:, j * tokens : (j + 1) * tokens] > 0.0, scaled, 0.0)
            coef_ref[:, j * tokens : (j + 1) * tokens] = coef.astype(BF16)
        rows = [
            iquery_ref[:, j * index_width : (j + 1) * index_width]
            for j in range(first, first + span)
        ]
        total = total + jnp.dot(
            coef_ref[:, first * tokens : (first + span) * tokens],
            jnp.concatenate(rows, axis=0),
            preferred_element_type=F32,
        )
    grad_ref[...] = total


def query_grad_kernel(blocks, *refs):
    coefs, diffs, actives, ikeys = (refs[i * blocks : (i + 1) * blocks] for i in range(4))
    grad_ref, weight_grad_ref = refs[4 * blocks :]
    tokens = diffs[0].shape[1]
    index_width = ikeys[0].shape[1]
    for j in range(weight_grad_ref.shape[0]):
        at = slice(j * tokens, (j + 1) * tokens)
        grad, weight_grad = 0.0, 0.0
        for coef, diff, active, ikey in zip(coefs, diffs, actives, ikeys):
            grad = grad + lax.dot_general(
                coef[:, at], ikey[...], (((0,), (0,)), ((), ())), preferred_element_type=F32
            )
            weight_grad = weight_grad + jnp.sum(diff[...] * active[:, at], axis=0, keepdims=True)
        grad_ref[:, j * index_width : (j + 1) * index_width] = grad
        weight_grad_ref[j : j + 1, :] = weight_grad


def body(
    attn_query, key_latent, lse_attn, index_query, index_key, index_weight, lse_index, block_order
):
    tokens, key_width = key_latent.shape
    index_width = index_key.shape[1]
    heads = attn_query.shape[1] // key_width
    iheads = index_query.shape[1] // index_width
    wide, narrow = lax.axis_size("wide"), lax.axis_size("narrow")
    ranks = range(wide * narrow)

    def send(block, step, flip, spread=False):
        route = []
        for r in ranks:
            turn = r % 2 * 2 if spread else flip
            route.append((r, (r // narrow - step) % wide * narrow + (r % narrow ^ turn)))
        return lax.ppermute(block, ("wide", "narrow"), route)

    like = jax.ShapeDtypeStruct
    hbm = pltpu.MemorySpace.HBM
    small = (
        jnp.transpose(key_latent),
        index_key,
        index_query,
        lse_attn,
        index_weight,
        lse_index[None, :],
    )
    half = (key_width + tokens) // 2
    packed, *small, mine, live = call(
        load_kernel,
        (like((key_width + tokens, tokens), BF16),)
        + tuple(like(a.shape, a.dtype) for a in small[2:])
        + (like((half, tokens), BF16), like((wide, 1, tokens), F32)),
        [pl.BlockSpec(memory_space=hbm)] * 7,
        [pltpu.SMEM(block_order.shape, jnp.int32), pltpu.SemaphoreType.DMA((7,))],
        limit=4 << 20,
    )(*(pltpu.with_memory_space_constraint(x, hbm) for x in (block_order, *small)))
    iquery, lse, weight, lse_row = small
    blocks = [None]
    for b in range(1, wide):
        first = send(mine, -b, 0)
        blocks.append((first, send(first, 0, 1)))

    part = like((2, tokens, tokens), F32)
    act = like((tokens, iheads * tokens), F32)
    work = dict(
        flops=2 * tokens * tokens * (heads * key_width + iheads * index_width),
        moved=attn_query.size * 2,
    )
    *own, turned, iturned = call(
        own_kernel,
        (
            part,
            act,
            like((heads * key_width, tokens), BF16),
            like((iheads * index_width, tokens), BF16),
        ),
        [pl.BlockSpec(memory_space=hbm)] + [vmem()] * 4,
        [
            pltpu.VMEM(attn_query.shape, BF16),
            pltpu.SemaphoreType.DMA((math.gcd(heads // 4, CHUNKS),)),
        ],
        limit=14 << 20,
        **work,
    )(pltpu.with_memory_space_constraint(attn_query, hbm), packed, iquery, lse, weight)
    other = call(
        other_kernel,
        (part, act, like(index_key.shape, BF16)),
        [vmem()] * 6,
        [pltpu.VMEM(packed.shape, BF16)],
        limit=10 << 20,
        **work,
    )
    found, ikeys = [own], [packed[key_width:]]
    for mine, theirs in blocks[1:]:
        *sums, ikey = other(turned, mine, theirs, lse, iturned, weight)
        found.append(sums)
        ikeys.append(ikey)
    sums = []
    for found_part, *_ in found:
        far = send(found_part.astype(BF16), 0, 2)
        summed = found_part + far.astype(F32)
        sums.append((summed, send(summed, 0, 1)))

    steps, grads = [], []
    for b in range(wide):
        grad_block = call(
            functools.partial(key_grad_kernel, b),
            (
                like((tokens, index_width), F32),
                like((tokens, iheads * tokens), BF16),
                like((tokens, tokens), F32),
            ),
            [vmem()] * 7,
            limit=8 << 20,
            flops=2 * tokens * tokens * iheads * index_width,
            moved=tokens * tokens * iheads * 6,
        )
        grad, coef, difference = grad_block(live, *sums[b], lse_row, found[b][1], weight, iquery)
        steps.append((coef, difference, found[b][1], ikeys[b]))
        if b:
            near = send(grad, 0, 1)
            grad = grad + near
        grads.append(grad.astype(BF16))

    far = send(grads[0], 0, 2)
    own_grad = grads[0].astype(F32) + far.astype(F32)
    shared = []
    for b in range(1, wide):
        shared.append(send(grads[b], b, 0, spread=True))
    own_grad = own_grad + send(own_grad, 0, 1)

    grad_query, grad_weight = call(
        functools.partial(query_grad_kernel, wide),
        (like((tokens, iheads * index_width), F32), like((iheads, tokens), F32)),
        [vmem()] * (4 * wide),
        limit=8 << 20,
        flops=2 * wide * tokens * tokens * iheads * index_width,
        moved=wide * tokens * tokens * iheads * 6,
    )(*(x for kind in zip(*steps) for x in kind))

    if wide == 1:
        return grad_query, grad_weight, own_grad
    shared = shared[0] if wide == 2 else sum(x.astype(F32) for x in shared)
    theirs = send(shared, 0, 1)
    return grad_query, grad_weight, own_grad + (shared.astype(F32) + theirs.astype(F32))


def solution(mesh):
    in_specs = (
        P(("seq", "wide"), "narrow"),
        P(("seq", "wide"), None),
        P("narrow", ("seq", "wide")),
        P(("seq", "wide"), "narrow"),
        P(("seq", "wide"), None),
        P("narrow", ("seq", "wide")),
        P(("seq", "wide")),
        P("seq"),
    )
    out_specs = (
        P(("seq", "wide"), "narrow"),
        P("narrow", ("seq", "wide")),
        P(("seq", "wide"), None),
    )
    return jax.shard_map(
        body,
        mesh=mesh,
        in_specs=in_specs,
        out_specs=out_specs,
        check_vma=False,
    )
```

time: 120 us -> 30.3 us (0.25)
  waiting for transfers between devices: 67.9 us -> 12.1 us
  between operations: 16.2 us -> 0.75 us
  matrix products: 13.6 us -> 0 us
  local copies, waits for them, and re-layouts: 12.4 us -> 0.01 us
  Pallas kernels: 0 us -> 8.82 us
  other arithmetic: 3.2 us -> 0.74 us
  starting transfers between devices: 6.27 us -> 7.78 us
    psum x2 -> x0, waiting for transfers between devices: 63.9 us -> none  [the longest x1 34.1 us: block_grads(): target, score = lax.psum((part_target, part_score), 'narrow')]
    dot_general x12 -> x0, matrix products: 13.6 us -> none  [the longest x2 6.66 us: block_grads(): jnp.einsum('thc,sc->ths', query_heads, key_block, preferred_element_type=...]
    unnamed x21 -> x0, local copies, waits for them, and re-layouts: 10.1 us -> none
    pallas_call x0 -> x6, Pallas kernels: none -> 8.82 us  [the longest x1 4.04 us: body(): call(own_kernel, (part, act, like((heads * key_width, tokens), BF16), lik...]
    ppermute x4 -> x11, waiting for transfers between devices: 4 us -> 12.1 us  [send(): return lax.ppermute(block, ('wide', 'narrow'), route)]
    ppermute x4 -> x11, starting transfers between devices: 6.19 us -> 7.78 us  [send(): return lax.ppermute(block, ('wide', 'narrow'), route)]
    dynamic_slice x1 -> x0, local copies, waits for them, and re-layouts: 1.36 us -> none  [block_grads(): key_pos = block_order[source] * tok_rows + offsets]
    div x2 -> x0, other arithmetic: 1.27 us -> none  [block_grads(): jnp.sum(jnp.exp(scores - lse_rows[:, :, None]), axis=1) / HEADS]
  transfers between devices with their start and end apart: 6 -> 11, of which waited for: 4 -> 6; matrix products, arithmetic and copies ran while one was open for 18% -> 0% of each run, Pallas kernels for 0% -> 25%
where the time goes in v2:
time: 30.3 us; the launch traced here: 30.2 us
  waiting for transfers between devices  12.1 us (40%)
  Pallas kernels  8.82 us (29%)
  starting transfers between devices  7.78 us (26%)
  between operations  0.75 us (2%)
  other arithmetic  0.74 us (2%)
    ppermute x11, waiting for transfers between devices, send(): return lax.ppermute(block, ('wide', 'narrow'), route)  12.1 us
    ppermute x11, starting transfers between devices, send(): return lax.ppermute(block, ('wide', 'narrow'), route)  7.78 us
    pallas_call x1, Pallas kernels, body(): call(own_kernel, (part, act, like((heads * key_width, tokens), BF16), lik...  4.04 us
    pallas_call x1, Pallas kernels, body(): call(functools.partial(query_grad_kernel, wide), (like((tokens, iheads *...  1.47 us
    pallas_call x1, Pallas kernels, body(): *sums, ikey = other(turned, mine, theirs, lse, iturned, weight)  1.23 us
    pallas_call x1, Pallas kernels, body(): call(load_kernel, (like((key_width + tokens, tokens), BF16),) + tuple((li...  1.22 us
    pallas_call x2, Pallas kernels, body(): grad_block(live, *sums[b], lse_row, found[b][1], weight, iquery)  0.85 us
    add x1, other arithmetic, body(): own_grad + (shared.astype(F32) + theirs.astype(F32))  0.65 us
  transfers between devices with their start and end apart: 11, of which 6 were waited for; matrix products, arithmetic and copies ran while one was open for 0% of the time, Pallas kernels for 25%

profile of v2, /device:TPU:0, one launch (start us, length us, event | category | flops | bytes accessed | tf_op | source)
XLA Modules:
  0.0 30.2 jit_solution(8422432388496419071)
XLA Ops:
  0.6 1.2 %shard_map.103 = (bf16[704,128]{1,0:T(8,128)(2,1)S(1)}, bf16[128,2048]{1,0:T(8,128)(2,1)S(1)}, f32[32,128]{1,0:T(8,128)S(1)}, f32[16,128]{1,0:T(8,128)S(1)}, f32...) custom-call(s32[2]{0:T(128)} %order_hbm.1, bf16[576,128]{1,0:T(8,128)(2,1)} %bitcast.2, ...), custom_call_target="tpu_custom_call" | custom-call | tf_op jit(solution)/shard_map/pallas_call | solution.py:229
  1.9 3.0 %collective-permute-start.2 = (bf16[352,128]{1,0:T(8,128)(2,1)S(1)}, bf16[352,128]{1,0:T(8,128)(2,1)S(1)}, u32[]{:S(2)}, u32[]{:S(2)}) collective-permute-start(bf16[352,128]{1,0:T(8,128)(2,1)S(1)} %get-tuple-element.35), channel_id=1, source_target_pairs={{0,16},{4,20},{8,24},{12,28},{16,0},{20,4},{24,8},{28,12},{1,17},{... | collective-permute-start | bytes 270344 | tf_op jit(solution)/shard_map/ppermute | solution.py:216
  4.9 2.6 %collective-permute-done.2.mine_ref = bf16[352,128]{1,0:T(8,128)(2,1)S(1)} collective-permute-done((bf16[352,128]{1,0:T(8,128)(2,1)S(1)}, bf16[352,128]{1,0:T(8,128)(2,1)S(1)}, u32[]{:S(2)}, u32[]{:S(2)}) %collective-permute-start.2) | collective-permute-done | bytes 90144 | tf_op jit(solution)/shard_map/ppermute | solution.py:216
  7.5 0.0 collective-permute-start.3
  7.5 4.0 %shard_map.104 = (f32[2,128,128]{2,1,0:T(8,128)S(1)}, f32[128,2048]{1,0:T(8,128)S(1)}, bf16[18432,128]{1,0:T(8,128)(2,1)S(1)}, bf16[2048,128]{1,0:T(8,128)(2,1)S(1)}) custom-call(bf16[128,18432]{1,0:T(8,128)(2,1)} %query_hbm.1, bf16[704,128]{1,0:T(8,128)(2,1)S(1)} %get-tuple-element.26.packed_ref, bf16[128,2048]{1,0:T(8,128)(2,1)S(1)} %get-tuple-element.27.iquery_ref, ...), custom_call_target="tpu_custom_call" | custom-call | flops 671088640 | bytes 4718592 | tf_op jit(solution)/shard_map/pallas_call | solution.py:250
  11.6 2.0 %collective-permute-start = (bf16[2,128,128]{2,1,0:T(8,128)(2,1)S(1)}, bf16[2,128,128]{2,1,0:T(8,128)(2,1)S(1)}, u32[]{:S(2)}, u32[]{:S(2)}) collective-permute-start(bf16[2,128,128]{2,1,0:T(8,128)(2,1)S(1)} %convert_element_type.30), channel_id=1, source_target_pairs={{0,8},{4,12},{8,0},{12,4},{16,24},{20,28},{24,16},{28,20},{1,9},{5... | collective-permute-start | bytes 196616 | tf_op jit(solution)/shard_map/ppermute | solution.py:216
  13.6 0.0 collective-permute-done.3.theirs_ref
  13.6 1.2 %shard_map.106 = (f32[2,128,128]{2,1,0:T(8,128)S(1)}, f32[128,2048]{1,0:T(8,128)S(1)}, bf16[128,128]{1,0:T(8,128)(2,1)S(1)}) custom-call(bf16[18432,128]{1,0:T(8,128)(2,1)S(1)} %get-tuple-element.34.turned_ref, bf16[352,128]{1,0:T(8,128)(2,1)S(1)} %collective-permute-done.2.mine_ref, bf16[352,128]{1,0:T(8,128)(2,1)S(1)} %collective-permute-done.3.theirs_ref, ...), custom_call_target="tpu_custom_call" | custom-call | flops 671088640 | bytes 4718592 | tf_op jit(solution)/shard_map/pallas_call | solution.py:276
  14.9 0.2 collective-permute-start.4
  15.0 1.3 %collective-permute-done = bf16[2,128,128]{2,1,0:T(8,128)(2,1)S(1)} collective-permute-done((bf16[2,128,128]{2,1,0:T(8,128)(2,1)S(1)}, bf16[2,128,128]{2,1,0:T(8,128)(2,1)S(1)}, u32[]{:S(2)}, u32[]{:S(2)}) %collective-permute-start) | collective-permute-done | bytes 65568 | tf_op jit(solution)/shard_map/ppermute | solution.py:216
  16.4 0.1 collective-permute-start.1
  16.4 2.7 %collective-permute-done.4 = bf16[2,128,128]{2,1,0:T(8,128)(2,1)S(1)} collective-permute-done((bf16[2,128,128]{2,1,0:T(8,128)(2,1)S(1)}, bf16[2,128,128]{2,1,0:T(8,128)(2,1)S(1)}, u32[]{:S(2)}, u32[]{:S(2)}) %collective-permute-start.4) | collective-permute-done | bytes 65568 | tf_op jit(solution)/shard_map/ppermute | solution.py:216
  19.2 0.1 collective-permute-start.5
  19.3 0.0 collective-permute-done.1.theirs_ref
  19.3 0.4 %shard_map.105 = (f32[128,128]{1,0:T(8,128)S(1)}, bf16[128,2048]{1,0:T(8,128)(2,1)S(1)}, f32[128,128]{1,0:T(8,128)S(1)}) custom-call(f32[2,1,128]{2,1,0:T(1,128)S(1)} %get-tuple-element.25.live_ref, f32[2,128,128]{2,1,0:T(8,128)S(1)} %convert_add_fusion.1.mine_ref, f32[2,128,128]{2,1,0:T(8,128)S(1)} %collective-permute-done.1.theirs_ref, ...), custom_call_target="tpu_custom_call" | custom-call | flops 67108864 | bytes 1572864 | tf_op jit(solution)/shard_map/pallas_call | solution.py:299
  19.7 0.4 %collective-permute-start.6 = (bf16[128,128]{1,0:T(8,128)(2,1)S(1)}, bf16[128,128]{1,0:T(8,128)(2,1)S(1)}, u32[]{:S(2)}, u32[]{:S(2)}) collective-permute-start(bf16[128,128]{1,0:T(8,128)(2,1)S(1)} %convert_element_type.34), channel_id=1, source_target_pairs={{0,8},{4,12},{8,0},{12,4},{16,24},{20,28},{24,16},{28,20},{1,9},{5... | collective-permute-start | bytes 98312 | tf_op jit(solution)/shard_map/ppermute | solution.py:216
  20.1 0.5 %collective-permute-done.5.theirs_ref = f32[2,128,128]{2,1,0:T(8,128)S(1)} collective-permute-done((f32[2,128,128]{2,1,0:T(8,128)S(1)}, f32[2,128,128]{2,1,0:T(8,128)S(1)}, u32[]{:S(2)}, u32[]{:S(2)}) %collective-permute-start.5) | collective-permute-done | bytes 131104 | tf_op jit(solution)/shard_map/ppermute | solution.py:216
  20.6 0.4 %shard_map.107 = (f32[128,128]{1,0:T(8,128)S(1)}, bf16[128,2048]{1,0:T(8,128)(2,1)S(1)}, f32[128,128]{1,0:T(8,128)S(1)}) custom-call(f32[2,1,128]{2,1,0:T(1,128)S(1)} %get-tuple-element.25.live_ref, f32[2,128,128]{2,1,0:T(8,128)S(1)} %convert_add_fusion.mine_ref, f32[2,128,128]{2,1,0:T(8,128)S(1)} %collective-permute-done.5.theirs_ref, ...), custom_call_target="tpu_custom_call" | custom-call | flops 67108864 | bytes 1572864 | tf_op jit(solution)/shard_map/pallas_call | solution.py:299
  21.1 0.2 collective-permute-start.8
  21.3 2.5 %collective-permute-done.6 = bf16[128,128]{1,0:T(8,128)(2,1)S(1)} collective-permute-done((bf16[128,128]{1,0:T(8,128)(2,1)S(1)}, bf16[128,128]{1,0:T(8,128)(2,1)S(1)}, u32[]{:S(2)}, u32[]{:S(2)}) %collective-permute-start.6) | collective-permute-done | bytes 32800 | tf_op jit(solution)/shard_map/ppermute | solution.py:216
  23.7 0.1 collective-permute-start.7
  23.8 0.0 collective-permute-done.8
  23.8 1.6 %collective-permute-start.9 = (bf16[128,128]{1,0:T(8,128)(2,1)S(1)}, bf16[128,128]{1,0:T(8,128)(2,1)S(1)}, u32[]{:S(2)}, u32[]{:S(2)}) collective-permute-start(bf16[128,128]{1,0:T(8,128)(2,1)S(1)} %add_convert_fusion), channel_id=1, source_target_pairs={{0,16},{4,28},{8,24},{12,20},{16,0},{20,12},{24,8},{28,4},{1,17},{... | collective-permute-start | bytes 98312 | tf_op jit(solution)/shard_map/ppermute | solution.py:216
  25.4 2.4 %collective-permute-done.9 = bf16[128,128]{1,0:T(8,128)(2,1)S(1)} collective-permute-done((bf16[128,128]{1,0:T(8,128)(2,1)S(1)}, bf16[128,128]{1,0:T(8,128)(2,1)S(1)}, u32[]{:S(2)}, u32[]{:S(2)}) %collective-permute-start.9) | collective-permute-done | bytes 32800 | tf_op jit(solution)/shard_map/ppermute | solution.py:216
  27.8 0.2 collective-permute-start.10
  28.1 1.5 %shard_map.108 = (f32[128,2048]{1,0:T(8,128)}, f32[16,128]{1,0:T(8,128)}) custom-call(bf16[128,2048]{1,0:T(8,128)(2,1)S(1)} %get-tuple-element.33.refs_0_, bf16[128,2048]{1,0:T(8,128)(2,1)S(1)} %get-tuple-element.39.refs_1_, f32[128,128]{1,0:T(8,128)S(1)} %get-tuple-element.40.refs_2_, f32[128,128]{1,0:T(8,128)S(1)} %get-tuple-element.41.refs_3_, ...), custom_call_target="tpu_custom_call" | custom-call | flops 134217728 | bytes 3145728 | tf_op jit(solution)/shard_map/pallas_call | solution.py:313
  29.5 0.0 collective-permute-done.7
  29.5 0.0 collective-permute-done.10
  29.5 0.7 %add_add_fusion = f32[128,128]{1,0:T(8,128)} fusion(bf16[128,128]{1,0:T(8,128)(2,1)S(1)} %collective-permute-done.10, bf16[128,128]{1,0:T(8,128)(2,1)S(1)} %collective-permute-done.9, f32[128,128]{1,0:T(8,128)S(1)} %collective-permute-done.7, bf16[128,128]{1,0:T(8,128)(2,1)S(1)} %collective-permute-done.6, f32[128,128]{1,0:T(8,128)S(1)} %get-tuple-element.45), kind=kLoop, calls=%fused_computation.2 | loop fusion | flops 147456 | bytes 294912 | tf_op jit(solution)/shard_map/add | solution.py:326
  (8 shorter events, 0.1 us)
Async XLA Ops:
  1.9 5.7 %collective-permute-start.2 = (bf16[352,128]{1,0:T(8,128)(2,1)S(1)}, bf16[352,128]{1,0:T(8,128)(2,1)S(1)}, u32[]{:S(2)}, u32[]{:S(2)}) collective-permute-start(bf16[352,128]{1,0:T(8,128)(2,1)S(1)} %get-tuple-element.35), channel_id=1, source_target_pairs={{0,16},{4,20},{8,24},{12,28},{16,0},{20,4},{24,8},{28,12},{1,17},{... | collective-permute-start | bytes 270344 | tf_op jit(solution)/shard_map/ppermute | solution.py:216
  7.5 6.1 %collective-permute-start.3 = (bf16[352,128]{1,0:T(8,128)(2,1)S(1)}, bf16[352,128]{1,0:T(8,128)(2,1)S(1)}, u32[]{:S(2)}, u32[]{:S(2)}) collective-permute-start(bf16[352,128]{1,0:T(8,128)(2,1)S(1)} %collective-permute-done.2.mine_ref), channel_id=1, source_target_pairs={{0,4},{4,0},{8,12},{12,8},{16,20},{20,16},{24,28},{28,24},{1,5},{5... | collective-permute-start | bytes 270344 | tf_op jit(solution)/shard_map/ppermute | solution.py:216
  11.6 4.8 %collective-permute-start = (bf16[2,128,128]{2,1,0:T(8,128)(2,1)S(1)}, bf16[2,128,128]{2,1,0:T(8,128)(2,1)S(1)}, u32[]{:S(2)}, u32[]{:S(2)}) collective-permute-start(bf16[2,128,128]{2,1,0:T(8,128)(2,1)S(1)} %convert_element_type.30), channel_id=1, source_target_pairs={{0,8},{4,12},{8,0},{12,4},{16,24},{20,28},{24,16},{28,20},{1,9},{5... | collective-permute-start | bytes 196616 | tf_op jit(solution)/shard_map/ppermute | solution.py:216
  14.9 4.3 %collective-permute-start.4 = (bf16[2,128,128]{2,1,0:T(8,128)(2,1)S(1)}, bf16[2,128,128]{2,1,0:T(8,128)(2,1)S(1)}, u32[]{:S(2)}, u32[]{:S(2)}) collective-permute-start(bf16[2,128,128]{2,1,0:T(8,128)(2,1)S(1)} %convert_element_type.32), channel_id=1, source_target_pairs={{0,8},{4,12},{8,0},{12,4},{16,24},{20,28},{24,16},{28,20},{1,9},{5... | collective-permute-start | bytes 196616 | tf_op jit(solution)/shard_map/ppermute | solution.py:216
  16.4 2.9 %collective-permute-start.1 = (f32[2,128,128]{2,1,0:T(8,128)S(1)}, f32[2,128,128]{2,1,0:T(8,128)S(1)}, u32[]{:S(2)}, u32[]{:S(2)}) collective-permute-start(f32[2,128,128]{2,1,0:T(8,128)S(1)} %convert_add_fusion.1.mine_ref), channel_id=1, source_target_pairs={{0,4},{4,0},{8,12},{12,8},{16,20},{20,16},{24,28},{28,24},{1,5},{5... | collective-permute-start | bytes 393224 | tf_op jit(solution)/shard_map/ppermute | solution.py:216
  19.2 1.4 %collective-permute-start.5 = (f32[2,128,128]{2,1,0:T(8,128)S(1)}, f32[2,128,128]{2,1,0:T(8,128)S(1)}, u32[]{:S(2)}, u32[]{:S(2)}) collective-permute-start(f32[2,128,128]{2,1,0:T(8,128)S(1)} %convert_add_fusion.mine_ref), channel_id=1, source_target_pairs={{0,4},{4,0},{8,12},{12,8},{16,20},{20,16},{24,28},{28,24},{1,5},{5... | collective-permute-start | bytes 393224 | tf_op jit(solution)/shard_map/ppermute | solution.py:216
  19.7 4.0 %collective-permute-start.6 = (bf16[128,128]{1,0:T(8,128)(2,1)S(1)}, bf16[128,128]{1,0:T(8,128)(2,1)S(1)}, u32[]{:S(2)}, u32[]{:S(2)}) collective-permute-start(bf16[128,128]{1,0:T(8,128)(2,1)S(1)} %convert_element_type.34), channel_id=1, source_target_pairs={{0,8},{4,12},{8,0},{12,4},{16,24},{20,28},{24,16},{28,20},{1,9},{5... | collective-permute-start | bytes 98312 | tf_op jit(solution)/shard_map/ppermute | solution.py:216
  21.1 2.8 %collective-permute-start.8 = (f32[128,128]{1,0:T(8,128)S(1)}, f32[128,128]{1,0:T(8,128)S(1)}, u32[]{:S(2)}, u32[]{:S(2)}) collective-permute-start(f32[128,128]{1,0:T(8,128)S(1)} %get-tuple-element.46), channel_id=1, source_target_pairs={{0,4},{4,0},{8,12},{12,8},{16,20},{20,16},{24,28},{28,24},{1,5},{5... | collective-permute-start | bytes 196616 | tf_op jit(solution)/shard_map/ppermute | solution.py:216
  23.7 5.8 %collective-permute-start.7 = (f32[128,128]{1,0:T(8,128)S(1)}, f32[128,128]{1,0:T(8,128)S(1)}, u32[]{:S(2)}, u32[]{:S(2)}) collective-permute-start(f32[128,128]{1,0:T(8,128)S(1)} %convert_add_fusion.2), channel_id=1, source_target_pairs={{0,4},{4,0},{8,12},{12,8},{16,20},{20,16},{24,28},{28,24},{1,5},{5... | collective-permute-start | bytes 196616 | tf_op jit(solution)/shard_map/ppermute | solution.py:216
  23.8 4.0 %collective-permute-start.9 = (bf16[128,128]{1,0:T(8,128)(2,1)S(1)}, bf16[128,128]{1,0:T(8,128)(2,1)S(1)}, u32[]{:S(2)}, u32[]{:S(2)}) collective-permute-start(bf16[128,128]{1,0:T(8,128)(2,1)S(1)} %add_convert_fusion), channel_id=1, source_target_pairs={{0,16},{4,28},{8,24},{12,20},{16,0},{20,12},{24,8},{28,4},{1,17},{... | collective-permute-start | bytes 98312 | tf_op jit(solution)/shard_map/ppermute | solution.py:216
  27.8 1.7 %collective-permute-start.10 = (bf16[128,128]{1,0:T(8,128)(2,1)S(1)}, bf16[128,128]{1,0:T(8,128)(2,1)S(1)}, u32[]{:S(2)}, u32[]{:S(2)}) collective-permute-start(bf16[128,128]{1,0:T(8,128)(2,1)S(1)} %collective-permute-done.9), channel_id=1, source_target_pairs={{0,4},{4,0},{8,12},{12,8},{16,20},{20,16},{24,28},{28,24},{1,5},{5... | collective-permute-start | bytes 98312 | tf_op jit(solution)/shard_map/ppermute | solution.py:216

commit v3 on v2

--- a/solution.py
+++ b/solution.py
@@ -11,7 +11,7 @@
 
 HEADS = 128
 SPAN = 8
-CHUNKS = 2
+CHUNKS = 4
 attn_scale = 192.0 ** (-0.5)
 F32 = jnp.float32
 BF16 = jnp.bfloat16
@@ -37,38 +37,54 @@
     return jnp.concatenate([ref[...] for ref in refs], axis=1)
 
 
-def block_sums(turned, packed, lse_ref, iturned_ref, weight_ref, part_ref, active_ref):
-    tokens = part_ref.shape[2]
-    heads, iheads = lse_ref.shape[0], weight_ref.shape[0]
+def index_sums(packed, iturned_ref, weight_ref, part_ref, active_ref):
+    tokens, iheads = part_ref.shape[2], weight_ref.shape[0]
     index_width = iturned_ref.shape[0] // iheads
     index_scale = index_width ** (-0.5)
-    width = packed.shape[0] - index_width
-    late = -width % 128
-    fill = jnp.zeros((late, packed.shape[1]), BF16)
-    sides = [
-        jnp.transpose(jnp.concatenate(parts, axis=0)) if late else jnp.transpose(packed[:width])
-        for parts in ((packed[:width], fill), (fill, packed[:width]))
-    ]
     score = 0.0
     for j in range(0, iheads, 2):
         rows = [iturned_ref.at[i * index_width : (i + 1) * index_width] for i in (j, j + 1)]
-        logits = jnp.dot(packed[width:], side_by_side(rows), preferred_element_type=F32)
+        logits = jnp.dot(
+            packed[packed.shape[0] - tokens :], side_by_side(rows), preferred_element_type=F32
+        )
         active = jnp.maximum(logits * index_scale, 0.0)
         active_ref[:, j * tokens : (j + 2) * tokens] = active
         for i in range(2):
             score = score + active[:, i * tokens : (i + 1) * tokens] * weight_ref[j + i : j + i + 1, :]
     part_ref[1] = score
 
+
+def key_sides(packed, tokens):
+    width = packed.shape[0] - tokens
+    late = -width % 128
+    if not late:
+        return [jnp.transpose(packed[:width])] * 2
+    fill = jnp.zeros((late, packed.shape[1]), BF16)
+    orders = ((packed[:width], fill), (fill, packed[:width]))
+    return [jnp.transpose(jnp.concatenate(parts, axis=0)) for parts in orders]
+
+
+def pair_scores(turned, p, keys, side):
+    pairs = [turned(p), turned(p + 1)]
+    first = side * (pairs[0].shape[0] - keys.shape[1])
+    rows = [pair.at[first : first + keys.shape[1]] for pair in pairs]
+    return jnp.dot(keys, side_by_side(rows), preferred_element_type=F32)
+
+
+def exp_sums(raw, p, side, lse_ref):
+    tokens, total = lse_ref.shape[1], 0.0
+    for i in range(2):
+        h = 2 * (p + i) + side
+        scores = raw[:, i * tokens : (i + 1) * tokens] * attn_scale
+        total = total + jnp.exp(scores - lse_ref[h : h + 1, :])
+    return total
+
+
+def target_sums(turned, sides, lse_ref, part_ref):
     total = 0.0
-    for p in range(0, heads // 2, 2):
-        pairs = [turned(p), turned(p + 1)]
+    for p in range(0, lse_ref.shape[0] // 2, 2):
         for side, keys in enumerate(sides):
-            first = side * (width - late)
-            rows = [pair.at[first : first + width + late] for pair in pairs]
-            both = jnp.dot(keys, side_by_side(rows), preferred_element_type=F32) * attn_scale
-            for i in range(2):
-                h = 2 * (p + i) + side
-                total = total + jnp.exp(both[:, i * tokens : (i + 1) * tokens] - lse_ref[h : h + 1, :])
+            total = total + exp_sums(pair_scores(turned, p, keys, side), p, side, lse_ref)
     part_ref[0] = total * (1.0 / HEADS)
 
 
@@ -100,31 +116,61 @@
 
 def own_kernel(
     query_hbm, packed_ref, iquery_ref, lse_ref, weight_ref,
-    part_ref, active_ref, turned_ref, iturned_ref, query_ref, sems,
+    part_ref, active_ref, turned_ref, iturned_ref, query_ref, raw_ref, sems,
 ):
     pair_width = query_ref.shape[1] // lse_ref.shape[0] * 2
+    tokens = part_ref.shape[2]
     step = query_ref.shape[1] // sems.shape[0]
     moves = []
     for i in range(sems.shape[0]):
         at = slice(i * step, (i + 1) * step)
         moves.append(pltpu.make_async_copy(query_hbm.at[:, at], query_ref.at[:, at], sems.at[i]))
-        moves[-1].start()
 
     def turned(p):
-        at = p * pair_width
-        if at % step == 0:
-            moves[at // step].wait()
-        at = slice(at, at + pair_width)
-        turned_ref[at] = jnp.transpose(query_ref[:, at])
-        return turned_ref.at[at]
-
-    @pl.when(lax.axis_index("wide") >= 0)
+        return turned_ref.at[p * pair_width : (p + 1) * pair_width]
+
+    always = lax.axis_index("wide") >= 0
+    moves[0].start()
+
+    @pl.when(always)
     def _():
         index_width = iquery_ref.shape[1] // weight_ref.shape[0]
         for j in range(weight_ref.shape[0]):
             at = slice(j * index_width, (j + 1) * index_width)
             iturned_ref[at] = jnp.transpose(iquery_ref[:, at])
-        block_sums(turned, packed_ref, lse_ref, iturned_ref, weight_ref, part_ref, active_ref)
+
+    for move in moves[1:2]:
+        move.start()
+
+    @pl.when(always)
+    def _():
+        index_sums(packed_ref, iturned_ref, weight_ref, part_ref, active_ref)
+
+    for move in moves[2:]:
+        move.start()
+
+    @pl.when(always)
+    def _():
+        sides = key_sides(packed_ref, tokens)
+        pairs = step // pair_width
+        total = 0.0
+        for i in range(len(moves) + 2):
+            if i < len(moves):
+                moves[i].wait()
+                for p in range(i * pairs, (i + 1) * pairs):
+                    at = slice(p * pair_width, (p + 1) * pair_width)
+                    turned_ref[at] = jnp.transpose(query_ref[:, at])
+            for lag in (1, 2):
+                if not 0 <= i - lag < len(moves):
+                    continue
+                slot = (i - lag) % 2
+                for k in range(pairs):
+                    p, side = (i - lag) * pairs + k // 2 * 2, k % 2
+                    if lag == 1:
+                        raw_ref[slot, k] = pair_scores(turned, p, sides[side], side)
+                    else:
+                        total = total + exp_sums(raw_ref[slot, k], p, side, lse_ref)
+        part_ref[0] = total * (1.0 / HEADS)
 
 
 def other_kernel(
@@ -141,7 +187,9 @@
     def turned(p):
         return turned_ref.at[p * pair_width : (p + 1) * pair_width]
 
-    block_sums(turned, packed_ref, lse_ref, iturned_ref, weight_ref, part_ref, active_ref)
+    sides = key_sides(packed_ref, part_ref.shape[2])
+    index_sums(packed_ref, iturned_ref, weight_ref, part_ref, active_ref)
+    target_sums(turned, sides, lse_ref, part_ref)
 
 
 def key_grad_kernel(
@@ -247,6 +295,7 @@
         flops=2 * tokens * tokens * (heads * key_width + iheads * index_width),
         moved=attn_query.size * 2,
     )
+    chunks = math.gcd(heads // 4, CHUNKS)
     *own, turned, iturned = call(
         own_kernel,
         (
@@ -258,7 +307,8 @@
         [pl.BlockSpec(memory_space=hbm)] + [vmem()] * 4,
         [
             pltpu.VMEM(attn_query.shape, BF16),
-            pltpu.SemaphoreType.DMA((math.gcd(heads // 4, CHUNKS),)),
+            pltpu.VMEM((2, heads // 2 // chunks, tokens, 2 * tokens), F32),
+            pltpu.SemaphoreType.DMA((chunks,)),
         ],
         limit=14 << 20,
         **work,

time: 30.3 us -> 29.8 us (0.983)
  Pallas kernels: 8.82 us -> 8.29 us
    pallas_call x1, Pallas kernels: 4.04 us -> 3.51 us  [body(): call(own_kernel, (part, act, like((heads * key_width, tokens), BF16), lik...]
  transfers between devices with their start and end apart: 11 -> 11, of which waited for: 6 -> 6; matrix products, arithmetic and copies ran while one was open for 0% -> 0% of each run, Pallas kernels for 25% -> 24%
where the time goes in v3:
time: 29.8 us; the launch traced here: 29.7 us
  waiting for transfers between devices  12.1 us (41%)
  Pallas kernels  8.29 us (28%)
  starting transfers between devices  7.79 us (26%)
  between operations  0.76 us (3%)
  other arithmetic  0.74 us (2%)
    ppermute x11, waiting for transfers between devices, send(): return lax.ppermute(block, ('wide', 'narrow'), route)  12.1 us
    ppermute x11, starting transfers between devices, send(): return lax.ppermute(block, ('wide', 'narrow'), route)  7.79 us
    pallas_call x1, Pallas kernels, body(): call(own_kernel, (part, act, like((heads * key_width, tokens), BF16), lik...  3.51 us
    pallas_call x1, Pallas kernels, body(): call(functools.partial(query_grad_kernel, wide), (like((tokens, iheads *...  1.47 us
    pallas_call x1, Pallas kernels, body(): *sums, ikey = other(turned, mine, theirs, lse, iturned, weight)  1.24 us
    pallas_call x1, Pallas kernels, body(): call(load_kernel, (like((key_width + tokens, tokens), BF16),) + tuple((li...  1.22 us
    pallas_call x2, Pallas kernels, body(): grad_block(live, *sums[b], lse_row, found[b][1], weight, iquery)  0.85 us
    add x1, other arithmetic, body(): own_grad + (shared.astype(F32) + theirs.astype(F32))  0.65 us
  transfers between devices with their start and end apart: 11, of which 6 were waited for; matrix products, arithmetic and copies ran while one was open for 0% of the time, Pallas kernels for 24%

profile of v3, /device:TPU:0, one launch (start us, length us, event | category | flops | bytes accessed | tf_op | source)
XLA Modules:
  0.0 29.7 jit_solution(10592321249720909924)
XLA Ops:
  0.6 1.2 %shard_map.103 = (bf16[704,128]{1,0:T(8,128)(2,1)S(1)}, bf16[128,2048]{1,0:T(8,128)(2,1)S(1)}, f32[32,128]{1,0:T(8,128)S(1)}, f32[16,128]{1,0:T(8,128)S(1)}, f32...) custom-call(s32[2]{0:T(128)} %order_hbm.1, bf16[576,128]{1,0:T(8,128)(2,1)} %bitcast.2, ...), custom_call_target="tpu_custom_call" | custom-call | tf_op jit(solution)/shard_map/pallas_call | solution.py:277
  1.9 3.0 %collective-permute-start.2 = (bf16[352,128]{1,0:T(8,128)(2,1)S(1)}, bf16[352,128]{1,0:T(8,128)(2,1)S(1)}, u32[]{:S(2)}, u32[]{:S(2)}) collective-permute-start(bf16[352,128]{1,0:T(8,128)(2,1)S(1)} %get-tuple-element.35), channel_id=1, source_target_pairs={{0,16},{4,20},{8,24},{12,28},{16,0},{20,4},{24,8},{28,12},{1,17},{... | collective-permute-start | bytes 270344 | tf_op jit(solution)/shard_map/ppermute | solution.py:264
  4.9 2.6 %collective-permute-done.2.mine_ref = bf16[352,128]{1,0:T(8,128)(2,1)S(1)} collective-permute-done((bf16[352,128]{1,0:T(8,128)(2,1)S(1)}, bf16[352,128]{1,0:T(8,128)(2,1)S(1)}, u32[]{:S(2)}, u32[]{:S(2)}) %collective-permute-start.2) | collective-permute-done | bytes 90144 | tf_op jit(solution)/shard_map/ppermute | solution.py:264
  7.5 0.0 collective-permute-start.3
  7.5 3.5 %shard_map.104 = (f32[2,128,128]{2,1,0:T(8,128)S(1)}, f32[128,2048]{1,0:T(8,128)S(1)}, bf16[18432,128]{1,0:T(8,128)(2,1)S(1)}, bf16[2048,128]{1,0:T(8,128)(2,1)S(1)}) custom-call(bf16[128,18432]{1,0:T(8,128)(2,1)} %query_hbm.1, bf16[704,128]{1,0:T(8,128)(2,1)S(1)} %get-tuple-element.26.packed_ref, bf16[128,2048]{1,0:T(8,128)(2,1)S(1)} %get-tuple-element.27.iquery_ref, ...), custom_call_target="tpu_custom_call" | custom-call | flops 671088640 | bytes 4718592 | tf_op jit(solution)/shard_map/pallas_call | solution.py:299
  11.1 2.0 %collective-permute-start = (bf16[2,128,128]{2,1,0:T(8,128)(2,1)S(1)}, bf16[2,128,128]{2,1,0:T(8,128)(2,1)S(1)}, u32[]{:S(2)}, u32[]{:S(2)}) collective-permute-start(bf16[2,128,128]{2,1,0:T(8,128)(2,1)S(1)} %convert_element_type.30), channel_id=1, source_target_pairs={{0,8},{4,12},{8,0},{12,4},{16,24},{20,28},{24,16},{28,20},{1,9},{5... | collective-permute-start | bytes 196616 | tf_op jit(solution)/shard_map/ppermute | solution.py:264
  13.1 0.0 collective-permute-done.3.theirs_ref
  13.1 1.2 %shard_map.106 = (f32[2,128,128]{2,1,0:T(8,128)S(1)}, f32[128,2048]{1,0:T(8,128)S(1)}, bf16[128,128]{1,0:T(8,128)(2,1)S(1)}) custom-call(bf16[18432,128]{1,0:T(8,128)(2,1)S(1)} %get-tuple-element.34.turned_ref, bf16[352,128]{1,0:T(8,128)(2,1)S(1)} %collective-permute-done.2.mine_ref, bf16[352,128]{1,0:T(8,128)(2,1)S(1)} %collective-permute-done.3.theirs_ref, ...), custom_call_target="tpu_custom_call" | custom-call | flops 671088640 | bytes 4718592 | tf_op jit(solution)/shard_map/pallas_call | solution.py:326
  14.3 0.2 collective-permute-start.4
  14.5 1.3 %collective-permute-done = bf16[2,128,128]{2,1,0:T(8,128)(2,1)S(1)} collective-permute-done((bf16[2,128,128]{2,1,0:T(8,128)(2,1)S(1)}, bf16[2,128,128]{2,1,0:T(8,128)(2,1)S(1)}, u32[]{:S(2)}, u32[]{:S(2)}) %collective-permute-start) | collective-permute-done | bytes 65568 | tf_op jit(solution)/shard_map/ppermute | solution.py:264
  15.8 0.1 collective-permute-start.1
  15.9 2.7 %collective-permute-done.4 = bf16[2,128,128]{2,1,0:T(8,128)(2,1)S(1)} collective-permute-done((bf16[2,128,128]{2,1,0:T(8,128)(2,1)S(1)}, bf16[2,128,128]{2,1,0:T(8,128)(2,1)S(1)}, u32[]{:S(2)}, u32[]{:S(2)}) %collective-permute-start.4) | collective-permute-done | bytes 65568 | tf_op jit(solution)/shard_map/ppermute | solution.py:264
  18.7 0.1 collective-permute-start.5
  18.8 0.0 collective-permute-done.1.theirs_ref
  18.8 0.4 %shard_map.105 = (f32[128,128]{1,0:T(8,128)S(1)}, bf16[128,2048]{1,0:T(8,128)(2,1)S(1)}, f32[128,128]{1,0:T(8,128)S(1)}) custom-call(f32[2,1,128]{2,1,0:T(1,128)S(1)} %get-tuple-element.25.live_ref, f32[2,128,128]{2,1,0:T(8,128)S(1)} %convert_add_fusion.1.mine_ref, f32[2,128,128]{2,1,0:T(8,128)S(1)} %collective-permute-done.1.theirs_ref, ...), custom_call_target="tpu_custom_call" | custom-call | flops 67108864 | bytes 1572864 | tf_op jit(solution)/shard_map/pallas_call | solution.py:349
  19.2 0.4 %collective-permute-start.6 = (bf16[128,128]{1,0:T(8,128)(2,1)S(1)}, bf16[128,128]{1,0:T(8,128)(2,1)S(1)}, u32[]{:S(2)}, u32[]{:S(2)}) collective-permute-start(bf16[128,128]{1,0:T(8,128)(2,1)S(1)} %convert_element_type.34), channel_id=1, source_target_pairs={{0,8},{4,12},{8,0},{12,4},{16,24},{20,28},{24,16},{28,20},{1,9},{5... | collective-permute-start | bytes 98312 | tf_op jit(solution)/shard_map/ppermute | solution.py:264
  19.6 0.5 %collective-permute-done.5.theirs_ref = f32[2,128,128]{2,1,0:T(8,128)S(1)} collective-permute-done((f32[2,128,128]{2,1,0:T(8,128)S(1)}, f32[2,128,128]{2,1,0:T(8,128)S(1)}, u32[]{:S(2)}, u32[]{:S(2)}) %collective-permute-start.5) | collective-permute-done | bytes 131104 | tf_op jit(solution)/shard_map/ppermute | solution.py:264
  20.1 0.4 %shard_map.107 = (f32[128,128]{1,0:T(8,128)S(1)}, bf16[128,2048]{1,0:T(8,128)(2,1)S(1)}, f32[128,128]{1,0:T(8,128)S(1)}) custom-call(f32[2,1,128]{2,1,0:T(1,128)S(1)} %get-tuple-element.25.live_ref, f32[2,128,128]{2,1,0:T(8,128)S(1)} %convert_add_fusion.mine_ref, f32[2,128,128]{2,1,0:T(8,128)S(1)} %collective-permute-done.5.theirs_ref, ...), custom_call_target="tpu_custom_call" | custom-call | flops 67108864 | bytes 1572864 | tf_op jit(solution)/shard_map/pallas_call | solution.py:349
  20.5 0.2 collective-permute-start.8
  20.7 2.5 %collective-permute-done.6 = bf16[128,128]{1,0:T(8,128)(2,1)S(1)} collective-permute-done((bf16[128,128]{1,0:T(8,128)(2,1)S(1)}, bf16[128,128]{1,0:T(8,128)(2,1)S(1)}, u32[]{:S(2)}, u32[]{:S(2)}) %collective-permute-start.6) | collective-permute-done | bytes 32800 | tf_op jit(solution)/shard_map/ppermute | solution.py:264
  23.2 0.1 collective-permute-start.7
  23.3 0.0 collective-permute-done.8
  23.3 1.6 %collective-permute-start.9 = (bf16[128,128]{1,0:T(8,128)(2,1)S(1)}, bf16[128,128]{1,0:T(8,128)(2,1)S(1)}, u32[]{:S(2)}, u32[]{:S(2)}) collective-permute-start(bf16[128,128]{1,0:T(8,128)(2,1)S(1)} %add_convert_fusion), channel_id=1, source_target_pairs={{0,16},{4,28},{8,24},{12,20},{16,0},{20,12},{24,8},{28,4},{1,17},{... | collective-permute-start | bytes 98312 | tf_op jit(solution)/shard_map/ppermute | solution.py:264
  24.9 2.4 %collective-permute-done.9 = bf16[128,128]{1,0:T(8,128)(2,1)S(1)} collective-permute-done((bf16[128,128]{1,0:T(8,128)(2,1)S(1)}, bf16[128,128]{1,0:T(8,128)(2,1)S(1)}, u32[]{:S(2)}, u32[]{:S(2)}) %collective-permute-start.9) | collective-permute-done | bytes 32800 | tf_op jit(solution)/shard_map/ppermute | solution.py:264
  27.3 0.2 collective-permute-start.10
  27.5 1.5 %shard_map.108 = (f32[128,2048]{1,0:T(8,128)}, f32[16,128]{1,0:T(8,128)}) custom-call(bf16[128,2048]{1,0:T(8,128)(2,1)S(1)} %get-tuple-element.33.refs_0_, bf16[128,2048]{1,0:T(8,128)(2,1)S(1)} %get-tuple-element.39.refs_1_, f32[128,128]{1,0:T(8,128)S(1)} %get-tuple-element.40.refs_2_, f32[128,128]{1,0:T(8,128)S(1)} %get-tuple-element.41.refs_3_, ...), custom_call_target="tpu_custom_call" | custom-call | flops 134217728 | bytes 3145728 | tf_op jit(solution)/shard_map/pallas_call | solution.py:363
  29.0 0.0 collective-permute-done.7
  29.0 0.0 collective-permute-done.10
  29.0 0.7 %add_add_fusion = f32[128,128]{1,0:T(8,128)} fusion(bf16[128,128]{1,0:T(8,128)(2,1)S(1)} %collective-permute-done.10, bf16[128,128]{1,0:T(8,128)(2,1)S(1)} %collective-permute-done.9, f32[128,128]{1,0:T(8,128)S(1)} %collective-permute-done.7, bf16[128,128]{1,0:T(8,128)(2,1)S(1)} %collective-permute-done.6, f32[128,128]{1,0:T(8,128)S(1)} %get-tuple-element.45), kind=kLoop, calls=%fused_computation.2 | loop fusion | flops 147456 | bytes 294912 | tf_op jit(solution)/shard_map/add | solution.py:376
  (8 shorter events, 0.1 us)
Async XLA Ops:
  1.9 5.7 %collective-permute-start.2 = (bf16[352,128]{1,0:T(8,128)(2,1)S(1)}, bf16[352,128]{1,0:T(8,128)(2,1)S(1)}, u32[]{:S(2)}, u32[]{:S(2)}) collective-permute-start(bf16[352,128]{1,0:T(8,128)(2,1)S(1)} %get-tuple-element.35), channel_id=1, source_target_pairs={{0,16},{4,20},{8,24},{12,28},{16,0},{20,4},{24,8},{28,12},{1,17},{... | collective-permute-start | bytes 270344 | tf_op jit(solution)/shard_map/ppermute | solution.py:264
  7.5 5.5 %collective-permute-start.3 = (bf16[352,128]{1,0:T(8,128)(2,1)S(1)}, bf16[352,128]{1,0:T(8,128)(2,1)S(1)}, u32[]{:S(2)}, u32[]{:S(2)}) collective-permute-start(bf16[352,128]{1,0:T(8,128)(2,1)S(1)} %collective-permute-done.2.mine_ref), channel_id=1, source_target_pairs={{0,4},{4,0},{8,12},{12,8},{16,20},{20,16},{24,28},{28,24},{1,5},{5... | collective-permute-start | bytes 270344 | tf_op jit(solution)/shard_map/ppermute | solution.py:264
  11.1 4.8 %collective-permute-start = (bf16[2,128,128]{2,1,0:T(8,128)(2,1)S(1)}, bf16[2,128,128]{2,1,0:T(8,128)(2,1)S(1)}, u32[]{:S(2)}, u32[]{:S(2)}) collective-permute-start(bf16[2,128,128]{2,1,0:T(8,128)(2,1)S(1)} %convert_element_type.30), channel_id=1, source_target_pairs={{0,8},{4,12},{8,0},{12,4},{16,24},{20,28},{24,16},{28,20},{1,9},{5... | collective-permute-start | bytes 196616 | tf_op jit(solution)/shard_map/ppermute | solution.py:264
  14.3 4.3 %collective-permute-start.4 = (bf16[2,128,128]{2,1,0:T(8,128)(2,1)S(1)}, bf16[2,128,128]{2,1,0:T(8,128)(2,1)S(1)}, u32[]{:S(2)}, u32[]{:S(2)}) collective-permute-start(bf16[2,128,128]{2,1,0:T(8,128)(2,1)S(1)} %convert_element_type.32), channel_id=1, source_target_pairs={{0,8},{4,12},{8,0},{12,4},{16,24},{20,28},{24,16},{28,20},{1,9},{5... | collective-permute-start | bytes 196616 | tf_op jit(solution)/shard_map/ppermute | solution.py:264
  15.8 2.9 %collective-permute-start.1 = (f32[2,128,128]{2,1,0:T(8,128)S(1)}, f32[2,128,128]{2,1,0:T(8,128)S(1)}, u32[]{:S(2)}, u32[]{:S(2)}) collective-permute-start(f32[2,128,128]{2,1,0:T(8,128)S(1)} %convert_add_fusion.1.mine_ref), channel_id=1, source_target_pairs={{0,4},{4,0},{8,12},{12,8},{16,20},{20,16},{24,28},{28,24},{1,5},{5... | collective-permute-start | bytes 393224 | tf_op jit(solution)/shard_map/ppermute | solution.py:264
  18.7 1.4 %collective-permute-start.5 = (f32[2,128,128]{2,1,0:T(8,128)S(1)}, f32[2,128,128]{2,1,0:T(8,128)S(1)}, u32[]{:S(2)}, u32[]{:S(2)}) collective-permute-start(f32[2,128,128]{2,1,0:T(8,128)S(1)} %convert_add_fusion.mine_ref), channel_id=1, source_target_pairs={{0,4},{4,0},{8,12},{12,8},{16,20},{20,16},{24,28},{28,24},{1,5},{5... | collective-permute-start | bytes 393224 | tf_op jit(solution)/shard_map/ppermute | solution.py:264
  19.2 4.0 %collective-permute-start.6 = (bf16[128,128]{1,0:T(8,128)(2,1)S(1)}, bf16[128,128]{1,0:T(8,128)(2,1)S(1)}, u32[]{:S(2)}, u32[]{:S(2)}) collective-permute-start(bf16[128,128]{1,0:T(8,128)(2,1)S(1)} %convert_element_type.34), channel_id=1, source_target_pairs={{0,8},{4,12},{8,0},{12,4},{16,24},{20,28},{24,16},{28,20},{1,9},{5... | collective-permute-start | bytes 98312 | tf_op jit(solution)/shard_map/ppermute | solution.py:264
  20.5 2.8 %collective-permute-start.8 = (f32[128,128]{1,0:T(8,128)S(1)}, f32[128,128]{1,0:T(8,128)S(1)}, u32[]{:S(2)}, u32[]{:S(2)}) collective-permute-start(f32[128,128]{1,0:T(8,128)S(1)} %get-tuple-element.46), channel_id=1, source_target_pairs={{0,4},{4,0},{8,12},{12,8},{16,20},{20,16},{24,28},{28,24},{1,5},{5... | collective-permute-start | bytes 196616 | tf_op jit(solution)/shard_map/ppermute | solution.py:264
  23.2 5.8 %collective-permute-start.7 = (f32[128,128]{1,0:T(8,128)S(1)}, f32[128,128]{1,0:T(8,128)S(1)}, u32[]{:S(2)}, u32[]{:S(2)}) collective-permute-start(f32[128,128]{1,0:T(8,128)S(1)} %convert_add_fusion.2), channel_id=1, source_target_pairs={{0,4},{4,0},{8,12},{12,8},{16,20},{20,16},{24,28},{28,24},{1,5},{5... | collective-permute-start | bytes 196616 | tf_op jit(solution)/shard_map/ppermute | solution.py:264
  23.3 4.0 %collective-permute-start.9 = (bf16[128,128]{1,0:T(8,128)(2,1)S(1)}, bf16[128,128]{1,0:T(8,128)(2,1)S(1)}, u32[]{:S(2)}, u32[]{:S(2)}) collective-permute-start(bf16[128,128]{1,0:T(8,128)(2,1)S(1)} %add_convert_fusion), channel_id=1, source_target_pairs={{0,16},{4,28},{8,24},{12,20},{16,0},{20,12},{24,8},{28,4},{1,17},{... | collective-permute-start | bytes 98312 | tf_op jit(solution)/shard_map/ppermute | solution.py:264
  27.3 1.7 %collective-permute-start.10 = (bf16[128,128]{1,0:T(8,128)(2,1)S(1)}, bf16[128,128]{1,0:T(8,128)(2,1)S(1)}, u32[]{:S(2)}, u32[]{:S(2)}) collective-permute-start(bf16[128,128]{1,0:T(8,128)(2,1)S(1)} %collective-permute-done.9), channel_id=1, source_target_pairs={{0,4},{4,0},{8,12},{12,8},{16,20},{20,16},{24,28},{28,24},{1,5},{5... | collective-permute-start | bytes 98312 | tf_op jit(solution)/shard_map/ppermute | solution.py:264

commit v4 on v3

--- a/solution.py
+++ b/solution.py
@@ -192,16 +192,41 @@
     target_sums(turned, sides, lse_ref, part_ref)
 
 
+def partner_kernel(
+    ikey_ref, active_ref, iquery_ref, their_iquery_ref, actives_ref, iqueries_ref
+):
+    tokens, index_width = iquery_ref.shape[0], ikey_ref.shape[1]
+    iheads = iquery_ref.shape[1] // index_width
+    core = lax.axis_index("narrow") % 2
+    iqueries_ref[core] = iquery_ref[...]
+    iqueries_ref[1 - core] = their_iquery_ref[...]
+    actives_ref[core] = active_ref[...]
+    for j in range(0, iheads, 2):
+        rows = [their_iquery_ref[:, i * index_width : (i + 1) * index_width] for i in (j, j + 1)]
+        logits = lax.dot_general(
+            ikey_ref[...],
+            jnp.concatenate(rows, axis=0),
+            (((1,), (1,)), ((), ())),
+            preferred_element_type=F32,
+        )
+        actives_ref[1 - core, :, j * tokens : (j + 2) * tokens] = logits
+
+
 def key_grad_kernel(
-    step, live_ref, mine_ref, theirs_ref, lse_ref, active_ref, weight_ref, iquery_ref,
-    grad_ref, coef_ref, diff_ref,
+    step, live_ref, mine_ref, theirs_ref, lse_ref, weight_ref, actives_ref, iqueries_ref,
+    grad_ref, coefs_ref, diff_ref,
 ):
-    keys, tokens = mine_ref.shape[1:]
+    keys, tokens = diff_ref.shape
     index_width = grad_ref.shape[1]
-    iheads = weight_ref.shape[0]
+    cores, iheads = coefs_ref.shape[0], coefs_ref.shape[2] // tokens
     index_scale = index_width ** (-0.5)
-    target = mine_ref[0] + theirs_ref[0]
-    score = mine_ref[1] + theirs_ref[1]
+    target = mine_ref[:keys] + theirs_ref[:keys]
+    score = mine_ref[keys : 2 * keys] + theirs_ref[keys : 2 * keys]
+    weights = [weight_ref[...] * index_scale]
+    if cores > 1:
+        first_core = lax.axis_index("narrow") % 2 == 0
+        weights.append(theirs_ref[2 * keys :] * index_scale)
+        weights = [jnp.where(first_core, *w) for w in (weights, weights[::-1])]
     if step == 0:
         key_at = lax.broadcasted_iota(jnp.int32, (keys, tokens), 0)
         query_at = lax.broadcasted_iota(jnp.int32, (keys, tokens), 1)
@@ -212,21 +237,23 @@
     diff_ref[...] = difference
     total = jnp.zeros((keys, index_width), F32)
     span = math.gcd(iheads, SPAN)
-    for first in range(0, iheads, span):
-        for j in range(first, first + span):
-            scaled = difference * (weight_ref[j : j + 1, :] * index_scale)
-            coef = jnp.where(active_ref[:, j * tokens : (j + 1) * tokens] > 0.0, scaled, 0.0)
-            coef_ref[:, j * tokens : (j + 1) * tokens] = coef.astype(BF16)
-        rows = [
-            iquery_ref[:, j * index_width : (j + 1) * index_width]
-            for j in range(first, first + span)
-        ]
-        total = total + jnp.dot(
-            coef_ref[:, first * tokens : (first + span) * tokens],
-            jnp.concatenate(rows, axis=0),
-            preferred_element_type=F32,
-        )
-    grad_ref[...] = total
+    for c in range(cores):
+        for first in range(0, iheads, span):
+            for j in range(first, first + span):
+                at = slice(j * tokens, (j + 1) * tokens)
+                scaled = difference * weights[c][j : j + 1, :]
+                coef = jnp.where(actives_ref[c, :, at] > 0.0, scaled, 0.0)
+                coefs_ref[c, :, at] = coef.astype(BF16)
+            rows = [
+                iqueries_ref[c, :, j * index_width : (j + 1) * index_width]
+                for j in range(first, first + span)
+            ]
+            total = total + jnp.dot(
+                coefs_ref[c, :, first * tokens : (first + span) * tokens],
+                jnp.concatenate(rows, axis=0),
+                preferred_element_type=F32,
+            )
+    grad_ref[...] = total.astype(BF16)
 
 
 def query_grad_kernel(blocks, *refs):
@@ -234,12 +261,13 @@
     grad_ref, weight_grad_ref = refs[4 * blocks :]
     tokens = diffs[0].shape[1]
     index_width = ikeys[0].shape[1]
+    core = lax.axis_index("narrow") % 2
     for j in range(weight_grad_ref.shape[0]):
         at = slice(j * tokens, (j + 1) * tokens)
         grad, weight_grad = 0.0, 0.0
         for coef, diff, active, ikey in zip(coefs, diffs, actives, ikeys):
             grad = grad + lax.dot_general(
-                coef[:, at], ikey[...], (((0,), (0,)), ((), ())), preferred_element_type=F32
+                coef[core if coef.shape[0] > 1 else 0, :, at], ikey[...], (((0,), (0,)), ((), ())), preferred_element_type=F32
             )
             weight_grad = weight_grad + jnp.sum(diff[...] * active[:, at], axis=0, keepdims=True)
         grad_ref[:, j * index_width : (j + 1) * index_width] = grad
@@ -256,11 +284,8 @@
     wide, narrow = lax.axis_size("wide"), lax.axis_size("narrow")
     ranks = range(wide * narrow)
 
-    def send(block, step, flip, spread=False):
-        route = []
-        for r in ranks:
-            turn = r % 2 * 2 if spread else flip
-            route.append((r, (r // narrow - step) % wide * narrow + (r % narrow ^ turn)))
+    def send(block, step, flip):
+        route = [(r, (r // narrow - step) % wide * narrow + (r % narrow ^ flip)) for r in ranks]
         return lax.ppermute(block, ("wide", "narrow"), route)
 
     like = jax.ShapeDtypeStruct
@@ -284,6 +309,7 @@
         limit=4 << 20,
     )(*(pltpu.with_memory_space_constraint(x, hbm) for x in (block_order, *small)))
     iquery, lse, weight, lse_row = small
+    their_iquery = send(index_query, 0, 1)
     blocks = [None]
     for b in range(1, wide):
         first = send(mine, -b, 0)
@@ -327,37 +353,54 @@
         found.append(sums)
         ikeys.append(ikey)
     sums = []
-    for found_part, *_ in found:
+    for b, (found_part, *_) in enumerate(found):
         far = send(found_part.astype(BF16), 0, 2)
-        summed = found_part + far.astype(F32)
+        summed = jnp.reshape(found_part + far.astype(F32), (2 * tokens, tokens))
+        if b:
+            summed = jnp.concatenate([summed, weight], axis=0)
         sums.append((summed, send(summed, 0, 1)))
 
     steps, grads = [], []
+    partner = call(
+        partner_kernel,
+        (
+            like((2, tokens, iheads * tokens), F32),
+            like((2, tokens, iheads * index_width), BF16),
+        ),
+        [vmem()] * 4,
+        limit=8 << 20,
+        flops=2 * tokens * tokens * iheads * index_width,
+        moved=tokens * tokens * iheads * 12,
+    )
     for b in range(wide):
+        if b:
+            both = partner(ikeys[b], found[b][1], iquery, their_iquery)
+        else:
+            both = (found[b][1][None], iquery[None])
+        cores = both[0].shape[0]
         grad_block = call(
             functools.partial(key_grad_kernel, b),
             (
-                like((tokens, index_width), F32),
-                like((tokens, iheads * tokens), BF16),
+                like((tokens, index_width), BF16),
+                like((cores, tokens, iheads * tokens), BF16),
                 like((tokens, tokens), F32),
             ),
             [vmem()] * 7,
             limit=8 << 20,
-            flops=2 * tokens * tokens * iheads * index_width,
-            moved=tokens * tokens * iheads * 6,
+            flops=2 * cores * tokens * tokens * iheads * index_width,
+            moved=cores * tokens * tokens * iheads * 6,
         )
-        grad, coef, difference = grad_block(live, *sums[b], lse_row, found[b][1], weight, iquery)
+        grad, coef, difference = grad_block(live, *sums[b], lse_row, weight, *both)
         steps.append((coef, difference, found[b][1], ikeys[b]))
-        if b:
-            near = send(grad, 0, 1)
-            grad = grad + near
-        grads.append(grad.astype(BF16))
+        grads.append(grad)
 
     far = send(grads[0], 0, 2)
     own_grad = grads[0].astype(F32) + far.astype(F32)
-    shared = []
+    others = 0.0
     for b in range(1, wide):
-        shared.append(send(grads[b], b, 0, spread=True))
+        cross = send(grads[b], b, 2)
+        near = send(grads[b], b, 0)
+        others = others + (near.astype(F32) + cross.astype(F32))
     own_grad = own_grad + send(own_grad, 0, 1)
 
     grad_query, grad_weight = call(
@@ -369,11 +412,7 @@
         moved=wide * tokens * tokens * iheads * 6,
     )(*(x for kind in zip(*steps) for x in kind))
 
-    if wide == 1:
-        return grad_query, grad_weight, own_grad
-    shared = shared[0] if wide == 2 else sum(x.astype(F32) for x in shared)
-    theirs = send(shared, 0, 1)
-    return grad_query, grad_weight, own_grad + (shared.astype(F32) + theirs.astype(F32))
+    return grad_query, grad_weight, own_grad + others
 
 
 def solution(mesh):

time: 29.8 us -> 27.6 us (0.926)
  waiting for transfers between devices: 12.1 us -> 7 us
  starting transfers between devices: 7.79 us -> 9.86 us
  Pallas kernels: 8.29 us -> 9.08 us
    ppermute x11, waiting for transfers between devices: 12.1 us -> 7 us  [send(): return lax.ppermute(block, ('wide', 'narrow'), route)]
    ppermute x11, starting transfers between devices: 7.79 us -> 9.86 us  [send(): return lax.ppermute(block, ('wide', 'narrow'), route)]
    pallas_call x2 -> x3, Pallas kernels: 0.85 us -> 1.58 us  [the longest x2 1.15 us: body(): grad, coef, difference = grad_block(live, *sums[b], lse_row, weight, *both)]
  transfers between devices with their start and end apart: 11 -> 11, of which waited for: 6 -> 4; matrix products, arithmetic and copies ran while one was open for 0% -> 0% of each run, Pallas kernels for 24% -> 29%
where the time goes in v4:
time: 27.6 us; the launch traced here: 27.4 us
  starting transfers between devices  9.86 us (36%)
  Pallas kernels  9.08 us (33%)
  waiting for transfers between devices  7 us (25%)
  between operations  0.76 us (3%)
  other arithmetic  0.74 us (3%)
    ppermute x11, starting transfers between devices, send(): return lax.ppermute(block, ('wide', 'narrow'), route)  9.86 us
    ppermute x11, waiting for transfers between devices, send(): return lax.ppermute(block, ('wide', 'narrow'), route)  7 us
    pallas_call x1, Pallas kernels, body(): call(own_kernel, (part, act, like((heads * key_width, tokens), BF16), lik...  3.55 us
    pallas_call x1, Pallas kernels, body(): call(functools.partial(query_grad_kernel, wide), (like((tokens, iheads *...  1.49 us
    pallas_call x1, Pallas kernels, body(): *sums, ikey = other(turned, mine, theirs, lse, iturned, weight)  1.23 us
    pallas_call x1, Pallas kernels, body(): call(load_kernel, (like((key_width + tokens, tokens), BF16),) + tuple((li...  1.22 us
    pallas_call x2, Pallas kernels, body(): grad, coef, difference = grad_block(live, *sums[b], lse_row, weight, *both)  1.15 us
    add x1, other arithmetic, body(): return (grad_query, grad_weight, own_grad + others)  0.65 us
  transfers between devices with their start and end apart: 11, of which 4 were waited for; matrix products, arithmetic and copies ran while one was open for 0% of the time, Pallas kernels for 29%

profile of v4, /device:TPU:0, one launch (start us, length us, event | category | flops | bytes accessed | tf_op | source)
XLA Modules:
  0.0 27.4 jit_solution(3232320893869496966)
XLA Ops:
  0.6 1.2 %shard_map.103 = (bf16[704,128]{1,0:T(8,128)(2,1)S(1)}, bf16[128,2048]{1,0:T(8,128)(2,1)S(1)}, f32[32,128]{1,0:T(8,128)S(1)}, f32[16,128]{1,0:T(8,128)S(1)}, f32...) custom-call(s32[2]{0:T(128)} %order_hbm.1, bf16[576,128]{1,0:T(8,128)(2,1)} %bitcast.11, ...), custom_call_target="tpu_custom_call" | custom-call | tf_op jit(solution)/shard_map/pallas_call | solution.py:302
  1.9 3.0 %collective-permute-start.2 = (bf16[352,128]{1,0:T(8,128)(2,1)S(1)}, bf16[352,128]{1,0:T(8,128)(2,1)S(1)}, u32[]{:S(2)}, u32[]{:S(2)}) collective-permute-start(bf16[352,128]{1,0:T(8,128)(2,1)S(1)} %get-tuple-element.37), channel_id=1, source_target_pairs={{0,16},{4,20},{8,24},{12,28},{16,0},{20,4},{24,8},{28,12},{1,17},{... | collective-permute-start | bytes 270344 | tf_op jit(solution)/shard_map/ppermute | solution.py:289
  4.9 0.0 copy-start
  4.9 3.6 %shard_map.104 = (f32[2,128,128]{2,1,0:T(8,128)S(1)}, f32[128,2048]{1,0:T(8,128)S(1)}, bf16[18432,128]{1,0:T(8,128)(2,1)S(1)}, bf16[2048,128]{1,0:T(8,128)(2,1)S(1)}) custom-call(bf16[128,18432]{1,0:T(8,128)(2,1)} %query_hbm.1, bf16[704,128]{1,0:T(8,128)(2,1)S(1)} %get-tuple-element.28.packed_ref, bf16[128,2048]{1,0:T(8,128)(2,1)S(1)} %get-tuple-element.29.iquery_ref, ...), custom_call_target="tpu_custom_call" | custom-call | flops 671088640 | bytes 4718592 | tf_op jit(solution)/shard_map/pallas_call | solution.py:325
  8.5 1.6 %collective-permute-start = (bf16[2,128,128]{2,1,0:T(8,128)(2,1)S(1)}, bf16[2,128,128]{2,1,0:T(8,128)(2,1)S(1)}, u32[]{:S(2)}, u32[]{:S(2)}) collective-permute-start(bf16[2,128,128]{2,1,0:T(8,128)(2,1)S(1)} %convert_element_type.24), channel_id=1, source_target_pairs={{0,8},{4,12},{8,0},{12,4},{16,24},{20,28},{24,16},{28,20},{1,9},{5... | collective-permute-start | bytes 196616 | tf_op jit(solution)/shard_map/ppermute | solution.py:289
  10.1 0.0 collective-permute-done.2.mine_ref
  10.1 0.0 collective-permute-start.3
  10.1 2.7 %collective-permute-done = bf16[2,128,128]{2,1,0:T(8,128)(2,1)S(1)} collective-permute-done((bf16[2,128,128]{2,1,0:T(8,128)(2,1)S(1)}, bf16[2,128,128]{2,1,0:T(8,128)(2,1)S(1)}, u32[]{:S(2)}, u32[]{:S(2)}) %collective-permute-start) | collective-permute-done | bytes 65568 | tf_op jit(solution)/shard_map/ppermute | solution.py:289
  12.8 0.1 collective-permute-start.1
  12.9 0.0 collective-permute-done.3.theirs_ref
  12.9 1.2 %shard_map.106 = (f32[2,128,128]{2,1,0:T(8,128)S(1)}, f32[128,2048]{1,0:T(8,128)S(1)}, bf16[128,128]{1,0:T(8,128)(2,1)S(1)}) custom-call(bf16[18432,128]{1,0:T(8,128)(2,1)S(1)} %get-tuple-element.36.turned_ref, bf16[352,128]{1,0:T(8,128)(2,1)S(1)} %collective-permute-done.2.mine_ref, bf16[352,128]{1,0:T(8,128)(2,1)S(1)} %collective-permute-done.3.theirs_ref, ...), custom_call_target="tpu_custom_call" | custom-call | flops 671088640 | bytes 4718592 | tf_op jit(solution)/shard_map/pallas_call | solution.py:352
  14.2 1.6 %collective-permute-start.4 = (bf16[2,128,128]{2,1,0:T(8,128)(2,1)S(1)}, bf16[2,128,128]{2,1,0:T(8,128)(2,1)S(1)}, u32[]{:S(2)}, u32[]{:S(2)}) collective-permute-start(bf16[2,128,128]{2,1,0:T(8,128)(2,1)S(1)} %convert_element_type.26), channel_id=1, source_target_pairs={{0,8},{4,12},{8,0},{12,4},{16,24},{20,28},{24,16},{28,20},{1,9},{5... | collective-permute-start | bytes 196616 | tf_op jit(solution)/shard_map/ppermute | solution.py:289
  15.8 0.0 copy-done
  15.8 0.2 collective-permute-start.6
  16.0 0.0 collective-permute-done.1.theirs_ref
  16.0 0.4 %shard_map.105 = (bf16[128,128]{1,0:T(8,128)(2,1)S(1)}, bf16[1,128,2048]{2,1,0:T(8,128)(2,1)S(1)}, f32[128,128]{1,0:T(8,128)S(1)}) custom-call(f32[2,1,128]{2,1,0:T(1,128)S(1)} %get-tuple-element.27.live_ref, f32[256,128]{1,0:T(8,128)S(1)} %bitcast.9, f32[256,128]{1,0:T(8,128)S(1)} %collective-permute-done.1.theirs_ref, ...), custom_call_target="tpu_custom_call" | custom-call | flops 67108864 | bytes 1572864 | tf_op jit(solution)/shard_map/pallas_call | solution.py:393
  16.4 0.6 %collective-permute-start.7 = (bf16[128,128]{1,0:T(8,128)(2,1)S(1)}, bf16[128,128]{1,0:T(8,128)(2,1)S(1)}, u32[]{:S(2)}, u32[]{:S(2)}) collective-permute-start(bf16[128,128]{1,0:T(8,128)(2,1)S(1)} %get-tuple-element.49), channel_id=1, source_target_pairs={{0,8},{4,12},{8,0},{12,4},{16,24},{20,28},{24,16},{28,20},{1,9},{5... | collective-permute-start | bytes 98312 | tf_op jit(solution)/shard_map/ppermute | solution.py:289
  17.0 1.8 %collective-permute-done.4 = bf16[2,128,128]{2,1,0:T(8,128)(2,1)S(1)} collective-permute-done((bf16[2,128,128]{2,1,0:T(8,128)(2,1)S(1)}, bf16[2,128,128]{2,1,0:T(8,128)(2,1)S(1)}, u32[]{:S(2)}, u32[]{:S(2)}) %collective-permute-start.4) | collective-permute-done | bytes 65568 | tf_op jit(solution)/shard_map/ppermute | solution.py:289
  18.8 0.1 collective-permute-start.5
  18.8 1.5 %collective-permute-done.7 = bf16[128,128]{1,0:T(8,128)(2,1)S(1)} collective-permute-done((bf16[128,128]{1,0:T(8,128)(2,1)S(1)}, bf16[128,128]{1,0:T(8,128)(2,1)S(1)}, u32[]{:S(2)}, u32[]{:S(2)}) %collective-permute-start.7) | collective-permute-done | bytes 32800 | tf_op jit(solution)/shard_map/ppermute | solution.py:289
  20.4 0.1 collective-permute-start.8
  20.5 0.0 collective-permute-done.6.their_iquery_ref
  20.5 0.4 %shard_map.107 = (f32[2,128,2048]{2,1,0:T(8,128)S(1)}, bf16[2,128,2048]{2,1,0:T(8,128)(2,1)S(1)}) custom-call(bf16[128,128]{1,0:T(8,128)(2,1)S(1)} %get-tuple-element.40.ikey_ref.refs_7_, f32[128,2048]{1,0:T(8,128)S(1)} %get-tuple-element.41.active_ref.refs_5_, bf16[128,2048]{1,0:T(8,128)(2,1)S(1)} %get-tuple-element.29.iquery_ref, ...), custom_call_target="tpu_custom_call" | custom-call | flops 67108864 | bytes 3145728 | tf_op jit(solution)/shard_map/pallas_call | solution.py:377
  20.9 0.0 collective-permute-done.5.theirs_ref
  20.9 0.7 %shard_map.108 = (bf16[128,128]{1,0:T(8,128)(2,1)S(1)}, bf16[2,128,2048]{2,1,0:T(8,128)(2,1)S(1)}, f32[128,128]{1,0:T(8,128)S(1)}) custom-call(f32[2,1,128]{2,1,0:T(1,128)S(1)} %get-tuple-element.27.live_ref, f32[272,128]{1,0:T(8,128)S(1)} %pad_maximum_fusion.mine_ref, f32[272,128]{1,0:T(8,128)S(1)} %collective-permute-done.5.theirs_ref, ...), custom_call_target="tpu_custom_call" | custom-call | flops 134217728 | bytes 3145728 | tf_op jit(solution)/shard_map/pallas_call | solution.py:393
  21.7 1.2 %collective-permute-start.10 = (bf16[128,128]{1,0:T(8,128)(2,1)S(1)}, bf16[128,128]{1,0:T(8,128)(2,1)S(1)}, u32[]{:S(2)}, u32[]{:S(2)}) collective-permute-start(bf16[128,128]{1,0:T(8,128)(2,1)S(1)} %get-tuple-element.50), channel_id=1, source_target_pairs={{0,24},{4,28},{8,16},{12,20},{16,8},{20,12},{24,0},{28,4},{1,25},{... | collective-permute-start | bytes 98312 | tf_op jit(solution)/shard_map/ppermute | solution.py:289
  22.8 1.5 %collective-permute-start.9 = (bf16[128,128]{1,0:T(8,128)(2,1)S(1)}, bf16[128,128]{1,0:T(8,128)(2,1)S(1)}, u32[]{:S(2)}, u32[]{:S(2)}) collective-permute-start(bf16[128,128]{1,0:T(8,128)(2,1)S(1)} %get-tuple-element.50), channel_id=1, source_target_pairs={{0,16},{4,20},{8,24},{12,28},{16,0},{20,4},{24,8},{28,12},{1,17},{... | collective-permute-start | bytes 98312 | tf_op jit(solution)/shard_map/ppermute | solution.py:289
  24.3 1.5 %shard_map.109 = (f32[128,2048]{1,0:T(8,128)}, f32[16,128]{1,0:T(8,128)}) custom-call(bf16[1,128,2048]{2,1,0:T(8,128)(2,1)S(1)} %get-tuple-element.35.refs_0_, bf16[2,128,2048]{2,1,0:T(8,128)(2,1)S(1)} %get-tuple-element.44.refs_1_, f32[128,128]{1,0:T(8,128)S(1)} %get-tuple-element.45.refs_2_, f32[128,128]{1,0:T(8,128)S(1)} %get-tuple-element.46.refs_3_, ...), custom_call_target="tpu_custom_call" | custom-call | flops 134217728 | bytes 3145728 | tf_op jit(solution)/shard_map/pallas_call | solution.py:406
  25.8 0.0 collective-permute-done.8
  25.8 1.0 %collective-permute-done.10 = bf16[128,128]{1,0:T(8,128)(2,1)S(1)} collective-permute-done((bf16[128,128]{1,0:T(8,128)(2,1)S(1)}, bf16[128,128]{1,0:T(8,128)(2,1)S(1)}, u32[]{:S(2)}, u32[]{:S(2)}) %collective-permute-start.10) | collective-permute-done | bytes 32800 | tf_op jit(solution)/shard_map/ppermute | solution.py:289
  26.8 0.0 collective-permute-done.9
  26.8 0.7 %add_add_fusion = f32[128,128]{1,0:T(8,128)} fusion(bf16[128,128]{1,0:T(8,128)(2,1)S(1)} %collective-permute-done.10, bf16[128,128]{1,0:T(8,128)(2,1)S(1)} %collective-permute-done.9, f32[128,128]{1,0:T(8,128)S(1)} %collective-permute-done.8, bf16[128,128]{1,0:T(8,128)(2,1)S(1)} %collective-permute-done.7, bf16[128,128]{1,0:T(8,128)(2,1)S(1)} %get-tuple-element.49), kind=kLoop, calls=%fused_computation.3 | loop fusion | flops 131072 | bytes 262144 | tf_op jit(solution)/shard_map/add | solution.py:415
  (7 shorter events, 0.1 us)
Async XLA Ops:
  1.9 8.2 %collective-permute-start.2 = (bf16[352,128]{1,0:T(8,128)(2,1)S(1)}, bf16[352,128]{1,0:T(8,128)(2,1)S(1)}, u32[]{:S(2)}, u32[]{:S(2)}) collective-permute-start(bf16[352,128]{1,0:T(8,128)(2,1)S(1)} %get-tuple-element.37), channel_id=1, source_target_pairs={{0,16},{4,20},{8,24},{12,28},{16,0},{20,4},{24,8},{28,12},{1,17},{... | collective-permute-start | bytes 270344 | tf_op jit(solution)/shard_map/ppermute | solution.py:289
  4.9 10.9 %copy-start = (bf16[128,2048]{1,0:T(8,128)(2,1)S(1)}, bf16[128,2048]{1,0:T(8,128)(2,1)}, u32[]{:S(2)}) copy-start(bf16[128,2048]{1,0:T(8,128)(2,1)} %refs_2_.1) | copy-start | bytes 1572868
  8.5 4.3 %collective-permute-start = (bf16[2,128,128]{2,1,0:T(8,128)(2,1)S(1)}, bf16[2,128,128]{2,1,0:T(8,128)(2,1)S(1)}, u32[]{:S(2)}, u32[]{:S(2)}) collective-permute-start(bf16[2,128,128]{2,1,0:T(8,128)(2,1)S(1)} %convert_element_type.24), channel_id=1, source_target_pairs={{0,8},{4,12},{8,0},{12,4},{16,24},{20,28},{24,16},{28,20},{1,9},{5... | collective-permute-start | bytes 196616 | tf_op jit(solution)/shard_map/ppermute | solution.py:289
  10.1 2.8 %collective-permute-start.3 = (bf16[352,128]{1,0:T(8,128)(2,1)S(1)}, bf16[352,128]{1,0:T(8,128)(2,1)S(1)}, u32[]{:S(2)}, u32[]{:S(2)}) collective-permute-start(bf16[352,128]{1,0:T(8,128)(2,1)S(1)} %collective-permute-done.2.mine_ref), channel_id=1, source_target_pairs={{0,4},{4,0},{8,12},{12,8},{16,20},{20,16},{24,28},{28,24},{1,5},{5... | collective-permute-start | bytes 270344 | tf_op jit(solution)/shard_map/ppermute | solution.py:289
  12.8 3.2 %collective-permute-start.1 = (f32[256,128]{1,0:T(8,128)S(1)}, f32[256,128]{1,0:T(8,128)S(1)}, u32[]{:S(2)}, u32[]{:S(2)}) collective-permute-start(f32[256,128]{1,0:T(8,128)S(1)} %bitcast.8), channel_id=1, source_target_pairs={{0,4},{4,0},{8,12},{12,8},{16,20},{20,16},{24,28},{28,24},{1,5},{5... | collective-permute-start | bytes 393224 | tf_op jit(solution)/shard_map/ppermute | solution.py:289
  14.2 4.6 %collective-permute-start.4 = (bf16[2,128,128]{2,1,0:T(8,128)(2,1)S(1)}, bf16[2,128,128]{2,1,0:T(8,128)(2,1)S(1)}, u32[]{:S(2)}, u32[]{:S(2)}) collective-permute-start(bf16[2,128,128]{2,1,0:T(8,128)(2,1)S(1)} %convert_element_type.26), channel_id=1, source_target_pairs={{0,8},{4,12},{8,0},{12,4},{16,24},{20,28},{24,16},{28,20},{1,9},{5... | collective-permute-start | bytes 196616 | tf_op jit(solution)/shard_map/ppermute | solution.py:289
  15.8 4.7 %collective-permute-start.6 = (bf16[128,2048]{1,0:T(8,128)(2,1)S(1)}, bf16[128,2048]{1,0:T(8,128)(2,1)S(1)}, u32[]{:S(2)}, u32[]{:S(2)}) collective-permute-start(bf16[128,2048]{1,0:T(8,128)(2,1)S(1)} %copy-done), channel_id=1, source_target_pairs={{0,4},{4,0},{8,12},{12,8},{16,20},{20,16},{24,28},{28,24},{1,5},{5... | collective-permute-start | bytes 1572872 | tf_op jit(solution)/shard_map/ppermute | solution.py:289
  16.4 4.0 %collective-permute-start.7 = (bf16[128,128]{1,0:T(8,128)(2,1)S(1)}, bf16[128,128]{1,0:T(8,128)(2,1)S(1)}, u32[]{:S(2)}, u32[]{:S(2)}) collective-permute-start(bf16[128,128]{1,0:T(8,128)(2,1)S(1)} %get-tuple-element.49), channel_id=1, source_target_pairs={{0,8},{4,12},{8,0},{12,4},{16,24},{20,28},{24,16},{28,20},{1,9},{5... | collective-permute-start | bytes 98312 | tf_op jit(solution)/shard_map/ppermute | solution.py:289
  18.8 2.2 %collective-permute-start.5 = (f32[272,128]{1,0:T(8,128)S(1)}, f32[272,128]{1,0:T(8,128)S(1)}, u32[]{:S(2)}, u32[]{:S(2)}) collective-permute-start(f32[272,128]{1,0:T(8,128)S(1)} %pad_maximum_fusion.mine_ref), channel_id=1, source_target_pairs={{0,4},{4,0},{8,12},{12,8},{16,20},{20,16},{24,28},{28,24},{1,5},{5... | collective-permute-start | bytes 417800 | tf_op jit(solution)/shard_map/ppermute | solution.py:289
  20.4 5.4 %collective-permute-start.8 = (f32[128,128]{1,0:T(8,128)S(1)}, f32[128,128]{1,0:T(8,128)S(1)}, u32[]{:S(2)}, u32[]{:S(2)}) collective-permute-start(f32[128,128]{1,0:T(8,128)S(1)} %convert_add_fusion.2), channel_id=1, source_target_pairs={{0,4},{4,0},{8,12},{12,8},{16,20},{20,16},{24,28},{28,24},{1,5},{5... | collective-permute-start | bytes 196616 | tf_op jit(solution)/shard_map/ppermute | solution.py:289
  21.7 5.1 %collective-permute-start.10 = (bf16[128,128]{1,0:T(8,128)(2,1)S(1)}, bf16[128,128]{1,0:T(8,128)(2,1)S(1)}, u32[]{:S(2)}, u32[]{:S(2)}) collective-permute-start(bf16[128,128]{1,0:T(8,128)(2,1)S(1)} %get-tuple-element.50), channel_id=1, source_target_pairs={{0,24},{4,28},{8,16},{12,20},{16,8},{20,12},{24,0},{28,4},{1,25},{... | collective-permute-start | bytes 98312 | tf_op jit(solution)/shard_map/ppermute | solution.py:289
  22.8 3.9 %collective-permute-start.9 = (bf16[128,128]{1,0:T(8,128)(2,1)S(1)}, bf16[128,128]{1,0:T(8,128)(2,1)S(1)}, u32[]{:S(2)}, u32[]{:S(2)}) collective-permute-start(bf16[128,128]{1,0:T(8,128)(2,1)S(1)} %get-tuple-element.50), channel_id=1, source_target_pairs={{0,16},{4,20},{8,24},{12,28},{16,0},{20,4},{24,8},{28,12},{1,17},{... | collective-permute-start | bytes 98312 | tf_op jit(solution)/shard_map/ppermute | solution.py:289

commit v5 on v4

--- a/solution.py
+++ b/solution.py
@@ -256,6 +256,16 @@
     grad_ref[...] = total.astype(BF16)
 
 
+def split(part):
+    high = lax.reduce_precision(part[1], 8, 7)
+    return jnp.stack([part[0], high, part[1] - high]).astype(BF16)
+
+
+def received(pieces):
+    pieces = pieces.astype(F32)
+    return jnp.stack([pieces[0], pieces[1] + pieces[2]])
+
+
 def query_grad_kernel(blocks, *refs):
     coefs, diffs, actives, ikeys = (refs[i * blocks : (i + 1) * blocks] for i in range(4))
     grad_ref, weight_grad_ref = refs[4 * blocks :]
@@ -354,8 +364,8 @@
         ikeys.append(ikey)
     sums = []
     for b, (found_part, *_) in enumerate(found):
-        far = send(found_part.astype(BF16), 0, 2)
-        summed = jnp.reshape(found_part + far.astype(F32), (2 * tokens, tokens))
+        far = received(send(split(found_part), 0, 2))
+        summed = jnp.reshape(found_part + far, (2 * tokens, tokens))
         if b:
             summed = jnp.concatenate([summed, weight], axis=0)
         sums.append((summed, send(summed, 0, 1)))

time: 27.6 us -> 29.2 us (1.058)
  waiting for transfers between devices: 7 us -> 8.73 us
    ppermute x11, waiting for transfers between devices: 7 us -> 8.73 us  [send(): return lax.ppermute(block, ('wide', 'narrow'), route)]
    ppermute x11, starting transfers between devices: 9.86 us -> 9.57 us  [send(): return lax.ppermute(block, ('wide', 'narrow'), route)]
  transfers between devices with their start and end apart: 11 -> 11, of which waited for: 4 -> 7; matrix products, arithmetic and copies ran while one was open for 0% -> 1% of each run, Pallas kernels for 29% -> 15%
where the time goes in v5:
time: 29.2 us; the launch traced here: 29 us
  starting transfers between devices  9.57 us (33%)
  Pallas kernels  9.04 us (31%)
  waiting for transfers between devices  8.73 us (30%)
  other arithmetic  0.82 us (3%)
  between operations  0.81 us (3%)
    ppermute x11, starting transfers between devices, send(): return lax.ppermute(block, ('wide', 'narrow'), route)  9.57 us
    ppermute x11, waiting for transfers between devices, send(): return lax.ppermute(block, ('wide', 'narrow'), route)  8.73 us
    pallas_call x1, Pallas kernels, body(): call(own_kernel, (part, act, like((heads * key_width, tokens), BF16), lik...  3.51 us
    pallas_call x1, Pallas kernels, body(): call(functools.partial(query_grad_kernel, wide), (like((tokens, iheads *...  1.49 us
    pallas_call x1, Pallas kernels, body(): *sums, ikey = other(turned, mine, theirs, lse, iturned, weight)  1.24 us
    pallas_call x1, Pallas kernels, body(): call(load_kernel, (like((key_width + tokens, tokens), BF16),) + tuple((li...  1.22 us
    pallas_call x2, Pallas kernels, body(): grad, coef, difference = grad_block(live, *sums[b], lse_row, weight, *both)  1.15 us
    add x1, other arithmetic, body(): return (grad_query, grad_weight, own_grad + others)  0.65 us
  transfers between devices with their start and end apart: 11, of which 7 were waited for; matrix products, arithmetic and copies ran while one was open for 1% of the time, Pallas kernels for 15%

profile of v5, /device:TPU:0, one launch (start us, length us, event | category | flops | bytes accessed | tf_op | source)
XLA Modules:
  0.0 29.0 jit_solution(17825048200056540773)
XLA Ops:
  0.6 1.2 %shard_map.103 = (bf16[704,128]{1,0:T(8,128)(2,1)S(1)}, bf16[128,2048]{1,0:T(8,128)(2,1)S(1)}, f32[32,128]{1,0:T(8,128)S(1)}, f32[16,128]{1,0:T(8,128)S(1)}, f32...) custom-call(s32[2]{0:T(128)} %order_hbm.1, bf16[576,128]{1,0:T(8,128)(2,1)} %bitcast.11, ...), custom_call_target="tpu_custom_call" | custom-call | tf_op jit(solution)/shard_map/pallas_call | solution.py:312
  1.9 3.5 %shard_map.104 = (f32[2,128,128]{2,1,0:T(8,128)S(1)}, f32[128,2048]{1,0:T(8,128)S(1)}, bf16[18432,128]{1,0:T(8,128)(2,1)S(1)}, bf16[2048,128]{1,0:T(8,128)(2,1)S(1)}) custom-call(bf16[128,18432]{1,0:T(8,128)(2,1)} %query_hbm.1, bf16[704,128]{1,0:T(8,128)(2,1)S(1)} %get-tuple-element.28.packed_ref, bf16[128,2048]{1,0:T(8,128)(2,1)S(1)} %get-tuple-element.29.iquery_ref, ...), custom_call_target="tpu_custom_call" | custom-call | flops 671088640 | bytes 4718592 | tf_op jit(solution)/shard_map/pallas_call | solution.py:335
  5.4 0.0 copy-start
  5.5 3.1 %collective-permute-start = (bf16[3,128,128]{2,1,0:T(8,128)(2,1)S(1)}, bf16[3,128,128]{2,1,0:T(8,128)(2,1)S(1)}, u32[]{:S(2)}, u32[]{:S(2)}) collective-permute-start(bf16[3,128,128]{2,1,0:T(8,128)(2,1)S(1)} %pad_maximum_fusion.1), channel_id=1, source_target_pairs={{0,8},{4,12},{8,0},{12,4},{16,24},{20,28},{24,16},{28,20},{1,9},{5... | collective-permute-start | bytes 294920 | tf_op jit(solution)/shard_map/ppermute | solution.py:299
  8.5 1.5 %collective-permute-start.2 = (bf16[352,128]{1,0:T(8,128)(2,1)S(1)}, bf16[352,128]{1,0:T(8,128)(2,1)S(1)}, u32[]{:S(2)}, u32[]{:S(2)}) collective-permute-start(bf16[352,128]{1,0:T(8,128)(2,1)S(1)} %get-tuple-element.37), channel_id=1, source_target_pairs={{0,16},{4,20},{8,24},{12,28},{16,0},{20,4},{24,8},{28,12},{1,17},{... | collective-permute-start | bytes 270344 | tf_op jit(solution)/shard_map/ppermute | solution.py:299
  10.0 3.0 %collective-permute-done.2.mine_ref = bf16[352,128]{1,0:T(8,128)(2,1)S(1)} collective-permute-done((bf16[352,128]{1,0:T(8,128)(2,1)S(1)}, bf16[352,128]{1,0:T(8,128)(2,1)S(1)}, u32[]{:S(2)}, u32[]{:S(2)}) %collective-permute-start.2) | collective-permute-done | bytes 90144 | tf_op jit(solution)/shard_map/ppermute | solution.py:299
  13.0 0.0 collective-permute-start.3
  13.0 0.0 collective-permute-done
  13.1 0.6 %collective-permute-start.1 = (f32[256,128]{1,0:T(8,128)S(1)}, f32[256,128]{1,0:T(8,128)S(1)}, u32[]{:S(2)}, u32[]{:S(2)}) collective-permute-start(f32[256,128]{1,0:T(8,128)S(1)} %bitcast.8), channel_id=1, source_target_pairs={{0,4},{4,0},{8,12},{12,8},{16,20},{20,16},{24,28},{28,24},{1,5},{5... | collective-permute-start | bytes 393224 | tf_op jit(solution)/shard_map/ppermute | solution.py:299
  13.7 0.6 %collective-permute-done.3.theirs_ref = bf16[352,128]{1,0:T(8,128)(2,1)S(1)} collective-permute-done((bf16[352,128]{1,0:T(8,128)(2,1)S(1)}, bf16[352,128]{1,0:T(8,128)(2,1)S(1)}, u32[]{:S(2)}, u32[]{:S(2)}) %collective-permute-start.3) | collective-permute-done | bytes 90144 | tf_op jit(solution)/shard_map/ppermute | solution.py:299
  14.3 1.2 %shard_map.106 = (f32[2,128,128]{2,1,0:T(8,128)S(1)}, f32[128,2048]{1,0:T(8,128)S(1)}, bf16[128,128]{1,0:T(8,128)(2,1)S(1)}) custom-call(bf16[18432,128]{1,0:T(8,128)(2,1)S(1)} %get-tuple-element.36.turned_ref, bf16[352,128]{1,0:T(8,128)(2,1)S(1)} %collective-permute-done.2.mine_ref, bf16[352,128]{1,0:T(8,128)(2,1)S(1)} %collective-permute-done.3.theirs_ref, ...), custom_call_target="tpu_custom_call" | custom-call | flops 671088640 | bytes 4718592 | tf_op jit(solution)/shard_map/pallas_call | solution.py:362
  15.6 0.1 collective-permute-start.4
  15.8 0.0 copy-done
  15.8 0.2 collective-permute-start.6
  15.9 0.0 collective-permute-done.1.theirs_ref
  16.0 0.4 %shard_map.105 = (bf16[128,128]{1,0:T(8,128)(2,1)S(1)}, bf16[1,128,2048]{2,1,0:T(8,128)(2,1)S(1)}, f32[128,128]{1,0:T(8,128)S(1)}) custom-call(f32[2,1,128]{2,1,0:T(1,128)S(1)} %get-tuple-element.27.live_ref, f32[256,128]{1,0:T(8,128)S(1)} %bitcast.9, f32[256,128]{1,0:T(8,128)S(1)} %collective-permute-done.1.theirs_ref, ...), custom_call_target="tpu_custom_call" | custom-call | flops 67108864 | bytes 1572864 | tf_op jit(solution)/shard_map/pallas_call | solution.py:403
  16.4 1.9 %collective-permute-start.7 = (bf16[128,128]{1,0:T(8,128)(2,1)S(1)}, bf16[128,128]{1,0:T(8,128)(2,1)S(1)}, u32[]{:S(2)}, u32[]{:S(2)}) collective-permute-start(bf16[128,128]{1,0:T(8,128)(2,1)S(1)} %get-tuple-element.49), channel_id=1, source_target_pairs={{0,8},{4,12},{8,0},{12,4},{16,24},{20,28},{24,16},{28,20},{1,9},{5... | collective-permute-start | bytes 98312 | tf_op jit(solution)/shard_map/ppermute | solution.py:299
  18.2 2.7 %collective-permute-done.4 = bf16[3,128,128]{2,1,0:T(8,128)(2,1)S(1)} collective-permute-done((bf16[3,128,128]{2,1,0:T(8,128)(2,1)S(1)}, bf16[3,128,128]{2,1,0:T(8,128)(2,1)S(1)}, u32[]{:S(2)}, u32[]{:S(2)}) %collective-permute-start.4) | collective-permute-done | bytes 98336 | tf_op jit(solution)/shard_map/ppermute | solution.py:299
  21.0 0.1 collective-permute-start.5
  21.1 0.2 collective-permute-done.7
  21.3 0.4 %collective-permute-start.8 = (f32[128,128]{1,0:T(8,128)S(1)}, f32[128,128]{1,0:T(8,128)S(1)}, u32[]{:S(2)}, u32[]{:S(2)}) collective-permute-start(f32[128,128]{1,0:T(8,128)S(1)} %convert_add_fusion), channel_id=1, source_target_pairs={{0,4},{4,0},{8,12},{12,8},{16,20},{20,16},{24,28},{28,24},{1,5},{5... | collective-permute-start | bytes 196616 | tf_op jit(solution)/shard_map/ppermute | solution.py:299
  21.7 0.0 collective-permute-done.6.their_iquery_ref
  21.7 0.4 %shard_map.107 = (f32[2,128,2048]{2,1,0:T(8,128)S(1)}, bf16[2,128,2048]{2,1,0:T(8,128)(2,1)S(1)}) custom-call(bf16[128,128]{1,0:T(8,128)(2,1)S(1)} %get-tuple-element.40.ikey_ref.refs_7_, f32[128,2048]{1,0:T(8,128)S(1)} %get-tuple-element.41.active_ref.refs_5_, bf16[128,2048]{1,0:T(8,128)(2,1)S(1)} %get-tuple-element.29.iquery_ref, ...), custom_call_target="tpu_custom_call" | custom-call | flops 67108864 | bytes 3145728 | tf_op jit(solution)/shard_map/pallas_call | solution.py:387
  22.1 0.3 %collective-permute-done.5.theirs_ref = f32[272,128]{1,0:T(8,128)S(1)} collective-permute-done((f32[272,128]{1,0:T(8,128)S(1)}, f32[272,128]{1,0:T(8,128)S(1)}, u32[]{:S(2)}, u32[]{:S(2)}) %collective-permute-start.5) | collective-permute-done | bytes 139296 | tf_op jit(solution)/shard_map/ppermute | solution.py:299
  22.4 0.7 %shard_map.108 = (bf16[128,128]{1,0:T(8,128)(2,1)S(1)}, bf16[2,128,2048]{2,1,0:T(8,128)(2,1)S(1)}, f32[128,128]{1,0:T(8,128)S(1)}) custom-call(f32[2,1,128]{2,1,0:T(1,128)S(1)} %get-tuple-element.27.live_ref, f32[272,128]{1,0:T(8,128)S(1)} %pad_maximum_fusion.mine_ref, f32[272,128]{1,0:T(8,128)S(1)} %collective-permute-done.5.theirs_ref, ...), custom_call_target="tpu_custom_call" | custom-call | flops 134217728 | bytes 3145728 | tf_op jit(solution)/shard_map/pallas_call | solution.py:403
  23.2 1.3 %collective-permute-start.10 = (bf16[128,128]{1,0:T(8,128)(2,1)S(1)}, bf16[128,128]{1,0:T(8,128)(2,1)S(1)}, u32[]{:S(2)}, u32[]{:S(2)}) collective-permute-start(bf16[128,128]{1,0:T(8,128)(2,1)S(1)} %get-tuple-element.50), channel_id=1, source_target_pairs={{0,24},{4,28},{8,16},{12,20},{16,8},{20,12},{24,0},{28,4},{1,25},{... | collective-permute-start | bytes 98312 | tf_op jit(solution)/shard_map/ppermute | solution.py:299
  24.4 0.5 %collective-permute-start.9 = (bf16[128,128]{1,0:T(8,128)(2,1)S(1)}, bf16[128,128]{1,0:T(8,128)(2,1)S(1)}, u32[]{:S(2)}, u32[]{:S(2)}) collective-permute-start(bf16[128,128]{1,0:T(8,128)(2,1)S(1)} %get-tuple-element.50), channel_id=1, source_target_pairs={{0,16},{4,20},{8,24},{12,28},{16,0},{20,4},{24,8},{28,12},{1,17},{... | collective-permute-start | bytes 98312 | tf_op jit(solution)/shard_map/ppermute | solution.py:299
  25.0 1.5 %shard_map.109 = (f32[128,2048]{1,0:T(8,128)}, f32[16,128]{1,0:T(8,128)}) custom-call(bf16[1,128,2048]{2,1,0:T(8,128)(2,1)S(1)} %get-tuple-element.35.refs_0_, bf16[2,128,2048]{2,1,0:T(8,128)(2,1)S(1)} %get-tuple-element.44.refs_1_, f32[128,128]{1,0:T(8,128)S(1)} %get-tuple-element.45.refs_2_, f32[128,128]{1,0:T(8,128)S(1)} %get-tuple-element.46.refs_3_, ...), custom_call_target="tpu_custom_call" | custom-call | flops 134217728 | bytes 3145728 | tf_op jit(solution)/shard_map/pallas_call | solution.py:416
  26.5 0.0 collective-permute-done.8
  26.5 1.6 %collective-permute-done.10 = bf16[128,128]{1,0:T(8,128)(2,1)S(1)} collective-permute-done((bf16[128,128]{1,0:T(8,128)(2,1)S(1)}, bf16[128,128]{1,0:T(8,128)(2,1)S(1)}, u32[]{:S(2)}, u32[]{:S(2)}) %collective-permute-start.10) | collective-permute-done | bytes 32800 | tf_op jit(solution)/shard_map/ppermute | solution.py:299
  28.0 0.3 %collective-permute-done.9 = bf16[128,128]{1,0:T(8,128)(2,1)S(1)} collective-permute-done((bf16[128,128]{1,0:T(8,128)(2,1)S(1)}, bf16[128,128]{1,0:T(8,128)(2,1)S(1)}, u32[]{:S(2)}, u32[]{:S(2)}) %collective-permute-start.9) | collective-permute-done | bytes 32800 | tf_op jit(solution)/shard_map/ppermute | solution.py:299
  28.4 0.7 %add_add_fusion = f32[128,128]{1,0:T(8,128)} fusion(bf16[128,128]{1,0:T(8,128)(2,1)S(1)} %collective-permute-done.10, bf16[128,128]{1,0:T(8,128)(2,1)S(1)} %collective-permute-done.9, f32[128,128]{1,0:T(8,128)S(1)} %collective-permute-done.8, bf16[128,128]{1,0:T(8,128)(2,1)S(1)} %collective-permute-done.7, bf16[128,128]{1,0:T(8,128)(2,1)S(1)} %get-tuple-element.49), kind=kLoop, calls=%fused_computation.15 | loop fusion | flops 131072 | bytes 262144 | tf_op jit(solution)/shard_map/add | solution.py:425
  (17 shorter events, 0.2 us)
Async XLA Ops:
  5.4 10.4 %copy-start = (bf16[128,2048]{1,0:T(8,128)(2,1)S(1)}, bf16[128,2048]{1,0:T(8,128)(2,1)}, u32[]{:S(2)}) copy-start(bf16[128,2048]{1,0:T(8,128)(2,1)} %refs_2_.1) | copy-start | bytes 1572868
  5.5 7.6 %collective-permute-start = (bf16[3,128,128]{2,1,0:T(8,128)(2,1)S(1)}, bf16[3,128,128]{2,1,0:T(8,128)(2,1)S(1)}, u32[]{:S(2)}, u32[]{:S(2)}) collective-permute-start(bf16[3,128,128]{2,1,0:T(8,128)(2,1)S(1)} %pad_maximum_fusion.1), channel_id=1, source_target_pairs={{0,8},{4,12},{8,0},{12,4},{16,24},{20,28},{24,16},{28,20},{1,9},{5... | collective-permute-start | bytes 294920 | tf_op jit(solution)/shard_map/ppermute | solution.py:299
  8.5 4.5 %collective-permute-start.2 = (bf16[352,128]{1,0:T(8,128)(2,1)S(1)}, bf16[352,128]{1,0:T(8,128)(2,1)S(1)}, u32[]{:S(2)}, u32[]{:S(2)}) collective-permute-start(bf16[352,128]{1,0:T(8,128)(2,1)S(1)} %get-tuple-element.37), channel_id=1, source_target_pairs={{0,16},{4,20},{8,24},{12,28},{16,0},{20,4},{24,8},{28,12},{1,17},{... | collective-permute-start | bytes 270344 | tf_op jit(solution)/shard_map/ppermute | solution.py:299
  13.0 1.3 %collective-permute-start.3 = (bf16[352,128]{1,0:T(8,128)(2,1)S(1)}, bf16[352,128]{1,0:T(8,128)(2,1)S(1)}, u32[]{:S(2)}, u32[]{:S(2)}) collective-permute-start(bf16[352,128]{1,0:T(8,128)(2,1)S(1)} %collective-permute-done.2.mine_ref), channel_id=1, source_target_pairs={{0,4},{4,0},{8,12},{12,8},{16,20},{20,16},{24,28},{28,24},{1,5},{5... | collective-permute-start | bytes 270344 | tf_op jit(solution)/shard_map/ppermute | solution.py:299
  13.1 2.8 %collective-permute-start.1 = (f32[256,128]{1,0:T(8,128)S(1)}, f32[256,128]{1,0:T(8,128)S(1)}, u32[]{:S(2)}, u32[]{:S(2)}) collective-permute-start(f32[256,128]{1,0:T(8,128)S(1)} %bitcast.8), channel_id=1, source_target_pairs={{0,4},{4,0},{8,12},{12,8},{16,20},{20,16},{24,28},{28,24},{1,5},{5... | collective-permute-start | bytes 393224 | tf_op jit(solution)/shard_map/ppermute | solution.py:299
  15.6 5.3 %collective-permute-start.4 = (bf16[3,128,128]{2,1,0:T(8,128)(2,1)S(1)}, bf16[3,128,128]{2,1,0:T(8,128)(2,1)S(1)}, u32[]{:S(2)}, u32[]{:S(2)}) collective-permute-start(bf16[3,128,128]{2,1,0:T(8,128)(2,1)S(1)} %pad_maximum_fusion.2), channel_id=1, source_target_pairs={{0,8},{4,12},{8,0},{12,4},{16,24},{20,28},{24,16},{28,20},{1,9},{5... | collective-permute-start | bytes 294920 | tf_op jit(solution)/shard_map/ppermute | solution.py:299
  15.8 5.9 %collective-permute-start.6 = (bf16[128,2048]{1,0:T(8,128)(2,1)S(1)}, bf16[128,2048]{1,0:T(8,128)(2,1)S(1)}, u32[]{:S(2)}, u32[]{:S(2)}) collective-permute-start(bf16[128,2048]{1,0:T(8,128)(2,1)S(1)} %copy-done), channel_id=1, source_target_pairs={{0,4},{4,0},{8,12},{12,8},{16,20},{20,16},{24,28},{28,24},{1,5},{5... | collective-permute-start | bytes 1572872 | tf_op jit(solution)/shard_map/ppermute | solution.py:299
  16.4 4.9 %collective-permute-start.7 = (bf16[128,128]{1,0:T(8,128)(2,1)S(1)}, bf16[128,128]{1,0:T(8,128)(2,1)S(1)}, u32[]{:S(2)}, u32[]{:S(2)}) collective-permute-start(bf16[128,128]{1,0:T(8,128)(2,1)S(1)} %get-tuple-element.49), channel_id=1, source_target_pairs={{0,8},{4,12},{8,0},{12,4},{16,24},{20,28},{24,16},{28,20},{1,9},{5... | collective-permute-start | bytes 98312 | tf_op jit(solution)/shard_map/ppermute | solution.py:299
  21.0 1.4 %collective-permute-start.5 = (f32[272,128]{1,0:T(8,128)S(1)}, f32[272,128]{1,0:T(8,128)S(1)}, u32[]{:S(2)}, u32[]{:S(2)}) collective-permute-start(f32[272,128]{1,0:T(8,128)S(1)} %pad_maximum_fusion.mine_ref), channel_id=1, source_target_pairs={{0,4},{4,0},{8,12},{12,8},{16,20},{20,16},{24,28},{28,24},{1,5},{5... | collective-permute-start | bytes 417800 | tf_op jit(solution)/shard_map/ppermute | solution.py:299
  21.3 5.2 %collective-permute-start.8 = (f32[128,128]{1,0:T(8,128)S(1)}, f32[128,128]{1,0:T(8,128)S(1)}, u32[]{:S(2)}, u32[]{:S(2)}) collective-permute-start(f32[128,128]{1,0:T(8,128)S(1)} %convert_add_fusion), channel_id=1, source_target_pairs={{0,4},{4,0},{8,12},{12,8},{16,20},{20,16},{24,28},{28,24},{1,5},{5... | collective-permute-start | bytes 196616 | tf_op jit(solution)/shard_map/ppermute | solution.py:299
  23.2 4.9 %collective-permute-start.10 = (bf16[128,128]{1,0:T(8,128)(2,1)S(1)}, bf16[128,128]{1,0:T(8,128)(2,1)S(1)}, u32[]{:S(2)}, u32[]{:S(2)}) collective-permute-start(bf16[128,128]{1,0:T(8,128)(2,1)S(1)} %get-tuple-element.50), channel_id=1, source_target_pairs={{0,24},{4,28},{8,16},{12,20},{16,8},{20,12},{24,0},{28,4},{1,25},{... | collective-permute-start | bytes 98312 | tf_op jit(solution)/shard_map/ppermute | solution.py:299
  24.4 3.9 %collective-permute-start.9 = (bf16[128,128]{1,0:T(8,128)(2,1)S(1)}, bf16[128,128]{1,0:T(8,128)(2,1)S(1)}, u32[]{:S(2)}, u32[]{:S(2)}) collective-permute-start(bf16[128,128]{1,0:T(8,128)(2,1)S(1)} %get-tuple-element.50), channel_id=1, source_target_pairs={{0,16},{4,20},{8,24},{12,28},{16,0},{20,4},{24,8},{28,12},{1,17},{... | collective-permute-start | bytes 98312 | tf_op jit(solution)/shard_map/ppermute | solution.py:299

commit v6 on v5

--- a/solution.py
+++ b/solution.py
@@ -261,11 +261,6 @@
     return jnp.stack([part[0], high, part[1] - high]).astype(BF16)
 
 
-def received(pieces):
-    pieces = pieces.astype(F32)
-    return jnp.stack([pieces[0], pieces[1] + pieces[2]])
-
-
 def query_grad_kernel(blocks, *refs):
     coefs, diffs, actives, ikeys = (refs[i * blocks : (i + 1) * blocks] for i in range(4))
     grad_ref, weight_grad_ref = refs[4 * blocks :]
@@ -364,10 +359,9 @@
         ikeys.append(ikey)
     sums = []
     for b, (found_part, *_) in enumerate(found):
-        far = received(send(split(found_part), 0, 2))
-        summed = jnp.reshape(found_part + far, (2 * tokens, tokens))
-        if b:
-            summed = jnp.concatenate([summed, weight], axis=0)
+        far = send(split(found_part), 0, 2).astype(F32)
+        rows = [found_part[0] + far[0], found_part[1] + (far[1] + far[2])]
+        summed = jnp.concatenate(rows + [weight] * (b > 0), axis=0)
         sums.append((summed, send(summed, 0, 1)))
 
     steps, grads = [], []

time: 29.2 us -> 29.2 us (level)
  transfers between devices with their start and end apart: 11 -> 11, of which waited for: 7 -> 7; matrix products, arithmetic and copies ran while one was open for 1% -> 0% of each run, Pallas kernels for 15% -> 15%
where the time goes in v6:
time: 29.2 us; the launch traced here: 29 us
  starting transfers between devices  9.57 us (33%)
  Pallas kernels  9.04 us (31%)
  waiting for transfers between devices  8.77 us (30%)
  other arithmetic  0.82 us (3%)
  between operations  0.79 us (3%)
    ppermute x11, starting transfers between devices, send(): return lax.ppermute(block, ('wide', 'narrow'), route)  9.57 us
    ppermute x11, waiting for transfers between devices, send(): return lax.ppermute(block, ('wide', 'narrow'), route)  8.77 us
    pallas_call x1, Pallas kernels, body(): call(own_kernel, (part, act, like((heads * key_width, tokens), BF16), lik...  3.51 us
    pallas_call x1, Pallas kernels, body(): call(functools.partial(query_grad_kernel, wide), (like((tokens, iheads *...  1.49 us
    pallas_call x1, Pallas kernels, body(): *sums, ikey = other(turned, mine, theirs, lse, iturned, weight)  1.24 us
    pallas_call x1, Pallas kernels, body(): call(load_kernel, (like((key_width + tokens, tokens), BF16),) + tuple((li...  1.22 us
    pallas_call x2, Pallas kernels, body(): grad, coef, difference = grad_block(live, *sums[b], lse_row, weight, *both)  1.15 us
    add x1, other arithmetic, body(): return (grad_query, grad_weight, own_grad + others)  0.65 us
  transfers between devices with their start and end apart: 11, of which 7 were waited for; matrix products, arithmetic and copies ran while one was open for 0% of the time, Pallas kernels for 15%

profile of v6, /device:TPU:0, one launch (start us, length us, event | category | flops | bytes accessed | tf_op | source)
XLA Modules:
  0.0 29.0 jit_solution(9683886327059881648)
XLA Ops:
  0.6 1.2 %shard_map.103 = (bf16[704,128]{1,0:T(8,128)(2,1)S(1)}, bf16[128,2048]{1,0:T(8,128)(2,1)S(1)}, f32[32,128]{1,0:T(8,128)S(1)}, f32[16,128]{1,0:T(8,128)S(1)}, f32...) custom-call(s32[2]{0:T(128)} %order_hbm.1, bf16[576,128]{1,0:T(8,128)(2,1)} %bitcast.14, ...), custom_call_target="tpu_custom_call" | custom-call | tf_op jit(solution)/shard_map/pallas_call | solution.py:307
  1.9 3.5 %shard_map.104 = (f32[2,128,128]{2,1,0:T(8,128)S(1)}, f32[128,2048]{1,0:T(8,128)S(1)}, bf16[18432,128]{1,0:T(8,128)(2,1)S(1)}, bf16[2048,128]{1,0:T(8,128)(2,1)S(1)}) custom-call(bf16[128,18432]{1,0:T(8,128)(2,1)} %query_hbm.1, bf16[704,128]{1,0:T(8,128)(2,1)S(1)} %get-tuple-element.28.packed_ref, bf16[128,2048]{1,0:T(8,128)(2,1)S(1)} %get-tuple-element.29.iquery_ref, ...), custom_call_target="tpu_custom_call" | custom-call | flops 671088640 | bytes 4718592 | tf_op jit(solution)/shard_map/pallas_call | solution.py:330
  5.4 0.0 copy-start
  5.5 3.1 %collective-permute-start = (bf16[3,128,128]{2,1,0:T(8,128)(2,1)S(1)}, bf16[3,128,128]{2,1,0:T(8,128)(2,1)S(1)}, u32[]{:S(2)}, u32[]{:S(2)}) collective-permute-start(bf16[3,128,128]{2,1,0:T(8,128)(2,1)S(1)} %pad_maximum_fusion.2), channel_id=1, source_target_pairs={{0,8},{4,12},{8,0},{12,4},{16,24},{20,28},{24,16},{28,20},{1,9},{5... | collective-permute-start | bytes 294920 | tf_op jit(solution)/shard_map/ppermute | solution.py:294
  8.5 1.5 %collective-permute-start.2 = (bf16[352,128]{1,0:T(8,128)(2,1)S(1)}, bf16[352,128]{1,0:T(8,128)(2,1)S(1)}, u32[]{:S(2)}, u32[]{:S(2)}) collective-permute-start(bf16[352,128]{1,0:T(8,128)(2,1)S(1)} %get-tuple-element.37), channel_id=1, source_target_pairs={{0,16},{4,20},{8,24},{12,28},{16,0},{20,4},{24,8},{28,12},{1,17},{... | collective-permute-start | bytes 270344 | tf_op jit(solution)/shard_map/ppermute | solution.py:294
  10.0 3.0 %collective-permute-done.2.mine_ref = bf16[352,128]{1,0:T(8,128)(2,1)S(1)} collective-permute-done((bf16[352,128]{1,0:T(8,128)(2,1)S(1)}, bf16[352,128]{1,0:T(8,128)(2,1)S(1)}, u32[]{:S(2)}, u32[]{:S(2)}) %collective-permute-start.2) | collective-permute-done | bytes 90144 | tf_op jit(solution)/shard_map/ppermute | solution.py:294
  13.0 0.0 collective-permute-start.3
  13.0 0.0 collective-permute-done
  13.1 0.6 %collective-permute-start.1 = (f32[256,128]{1,0:T(8,128)S(1)}, f32[256,128]{1,0:T(8,128)S(1)}, u32[]{:S(2)}, u32[]{:S(2)}) collective-permute-start(f32[256,128]{1,0:T(8,128)S(1)} %pad_maximum_fusion.1.mine_ref), channel_id=1, source_target_pairs={{0,4},{4,0},{8,12},{12,8},{16,20},{20,16},{24,28},{28,24},{1,5},{5... | collective-permute-start | bytes 393224 | tf_op jit(solution)/shard_map/ppermute | solution.py:294
  13.7 0.6 %collective-permute-done.3.theirs_ref = bf16[352,128]{1,0:T(8,128)(2,1)S(1)} collective-permute-done((bf16[352,128]{1,0:T(8,128)(2,1)S(1)}, bf16[352,128]{1,0:T(8,128)(2,1)S(1)}, u32[]{:S(2)}, u32[]{:S(2)}) %collective-permute-start.3) | collective-permute-done | bytes 90144 | tf_op jit(solution)/shard_map/ppermute | solution.py:294
  14.3 1.2 %shard_map.106 = (f32[2,128,128]{2,1,0:T(8,128)S(1)}, f32[128,2048]{1,0:T(8,128)S(1)}, bf16[128,128]{1,0:T(8,128)(2,1)S(1)}) custom-call(bf16[18432,128]{1,0:T(8,128)(2,1)S(1)} %get-tuple-element.36.turned_ref, bf16[352,128]{1,0:T(8,128)(2,1)S(1)} %collective-permute-done.2.mine_ref, bf16[352,128]{1,0:T(8,128)(2,1)S(1)} %collective-permute-done.3.theirs_ref, ...), custom_call_target="tpu_custom_call" | custom-call | flops 671088640 | bytes 4718592 | tf_op jit(solution)/shard_map/pallas_call | solution.py:357
  15.6 0.1 collective-permute-start.4
  15.8 0.0 copy-done
  15.8 0.2 collective-permute-start.6
  15.9 0.0 collective-permute-done.1.theirs_ref
  16.0 0.4 %shard_map.105 = (bf16[128,128]{1,0:T(8,128)(2,1)S(1)}, bf16[1,128,2048]{2,1,0:T(8,128)(2,1)S(1)}, f32[128,128]{1,0:T(8,128)S(1)}) custom-call(f32[2,1,128]{2,1,0:T(1,128)S(1)} %get-tuple-element.27.live_ref, f32[256,128]{1,0:T(8,128)S(1)} %pad_maximum_fusion.1.mine_ref, f32[256,128]{1,0:T(8,128)S(1)} %collective-permute-done.1.theirs_ref, ...), custom_call_target="tpu_custom_call" | custom-call | flops 67108864 | bytes 1572864 | tf_op jit(solution)/shard_map/pallas_call | solution.py:397
  16.4 1.9 %collective-permute-start.7 = (bf16[128,128]{1,0:T(8,128)(2,1)S(1)}, bf16[128,128]{1,0:T(8,128)(2,1)S(1)}, u32[]{:S(2)}, u32[]{:S(2)}) collective-permute-start(bf16[128,128]{1,0:T(8,128)(2,1)S(1)} %get-tuple-element.49), channel_id=1, source_target_pairs={{0,8},{4,12},{8,0},{12,4},{16,24},{20,28},{24,16},{28,20},{1,9},{5... | collective-permute-start | bytes 98312 | tf_op jit(solution)/shard_map/ppermute | solution.py:294
  18.2 2.7 %collective-permute-done.4 = bf16[3,128,128]{2,1,0:T(8,128)(2,1)S(1)} collective-permute-done((bf16[3,128,128]{2,1,0:T(8,128)(2,1)S(1)}, bf16[3,128,128]{2,1,0:T(8,128)(2,1)S(1)}, u32[]{:S(2)}, u32[]{:S(2)}) %collective-permute-start.4) | collective-permute-done | bytes 98336 | tf_op jit(solution)/shard_map/ppermute | solution.py:294
  21.0 0.1 collective-permute-start.5
  21.1 0.2 collective-permute-done.7
  21.3 0.4 %collective-permute-start.8 = (f32[128,128]{1,0:T(8,128)S(1)}, f32[128,128]{1,0:T(8,128)S(1)}, u32[]{:S(2)}, u32[]{:S(2)}) collective-permute-start(f32[128,128]{1,0:T(8,128)S(1)} %convert_add_fusion), channel_id=1, source_target_pairs={{0,4},{4,0},{8,12},{12,8},{16,20},{20,16},{24,28},{28,24},{1,5},{5... | collective-permute-start | bytes 196616 | tf_op jit(solution)/shard_map/ppermute | solution.py:294
  21.6 0.0 collective-permute-done.6.their_iquery_ref
  21.6 0.4 %shard_map.107 = (f32[2,128,2048]{2,1,0:T(8,128)S(1)}, bf16[2,128,2048]{2,1,0:T(8,128)(2,1)S(1)}) custom-call(bf16[128,128]{1,0:T(8,128)(2,1)S(1)} %get-tuple-element.40.ikey_ref.refs_7_, f32[128,2048]{1,0:T(8,128)S(1)} %get-tuple-element.41.active_ref.refs_5_, bf16[128,2048]{1,0:T(8,128)(2,1)S(1)} %get-tuple-element.29.iquery_ref, ...), custom_call_target="tpu_custom_call" | custom-call | flops 67108864 | bytes 3145728 | tf_op jit(solution)/shard_map/pallas_call | solution.py:381
  22.1 0.3 %collective-permute-done.5.theirs_ref = f32[272,128]{1,0:T(8,128)S(1)} collective-permute-done((f32[272,128]{1,0:T(8,128)S(1)}, f32[272,128]{1,0:T(8,128)S(1)}, u32[]{:S(2)}, u32[]{:S(2)}) %collective-permute-start.5) | collective-permute-done | bytes 139296 | tf_op jit(solution)/shard_map/ppermute | solution.py:294
  22.4 0.7 %shard_map.108 = (bf16[128,128]{1,0:T(8,128)(2,1)S(1)}, bf16[2,128,2048]{2,1,0:T(8,128)(2,1)S(1)}, f32[128,128]{1,0:T(8,128)S(1)}) custom-call(f32[2,1,128]{2,1,0:T(1,128)S(1)} %get-tuple-element.27.live_ref, f32[272,128]{1,0:T(8,128)S(1)} %pad_maximum_fusion.mine_ref, f32[272,128]{1,0:T(8,128)S(1)} %collective-permute-done.5.theirs_ref, ...), custom_call_target="tpu_custom_call" | custom-call | flops 134217728 | bytes 3145728 | tf_op jit(solution)/shard_map/pallas_call | solution.py:397
  23.1 1.3 %collective-permute-start.10 = (bf16[128,128]{1,0:T(8,128)(2,1)S(1)}, bf16[128,128]{1,0:T(8,128)(2,1)S(1)}, u32[]{:S(2)}, u32[]{:S(2)}) collective-permute-start(bf16[128,128]{1,0:T(8,128)(2,1)S(1)} %get-tuple-element.50), channel_id=1, source_target_pairs={{0,24},{4,28},{8,16},{12,20},{16,8},{20,12},{24,0},{28,4},{1,25},{... | collective-permute-start | bytes 98312 | tf_op jit(solution)/shard_map/ppermute | solution.py:294
  24.4 0.5 %collective-permute-start.9 = (bf16[128,128]{1,0:T(8,128)(2,1)S(1)}, bf16[128,128]{1,0:T(8,128)(2,1)S(1)}, u32[]{:S(2)}, u32[]{:S(2)}) collective-permute-start(bf16[128,128]{1,0:T(8,128)(2,1)S(1)} %get-tuple-element.50), channel_id=1, source_target_pairs={{0,16},{4,20},{8,24},{12,28},{16,0},{20,4},{24,8},{28,12},{1,17},{... | collective-permute-start | bytes 98312 | tf_op jit(solution)/shard_map/ppermute | solution.py:294
  25.0 1.5 %shard_map.109 = (f32[128,2048]{1,0:T(8,128)}, f32[16,128]{1,0:T(8,128)}) custom-call(bf16[1,128,2048]{2,1,0:T(8,128)(2,1)S(1)} %get-tuple-element.35.refs_0_, bf16[2,128,2048]{2,1,0:T(8,128)(2,1)S(1)} %get-tuple-element.44.refs_1_, f32[128,128]{1,0:T(8,128)S(1)} %get-tuple-element.45.refs_2_, f32[128,128]{1,0:T(8,128)S(1)} %get-tuple-element.46.refs_3_, ...), custom_call_target="tpu_custom_call" | custom-call | flops 134217728 | bytes 3145728 | tf_op jit(solution)/shard_map/pallas_call | solution.py:410
  26.5 0.0 collective-permute-done.8
  26.5 1.5 %collective-permute-done.10 = bf16[128,128]{1,0:T(8,128)(2,1)S(1)} collective-permute-done((bf16[128,128]{1,0:T(8,128)(2,1)S(1)}, bf16[128,128]{1,0:T(8,128)(2,1)S(1)}, u32[]{:S(2)}, u32[]{:S(2)}) %collective-permute-start.10) | collective-permute-done | bytes 32800 | tf_op jit(solution)/shard_map/ppermute | solution.py:294
  28.0 0.3 %collective-permute-done.9 = bf16[128,128]{1,0:T(8,128)(2,1)S(1)} collective-permute-done((bf16[128,128]{1,0:T(8,128)(2,1)S(1)}, bf16[128,128]{1,0:T(8,128)(2,1)S(1)}, u32[]{:S(2)}, u32[]{:S(2)}) %collective-permute-start.9) | collective-permute-done | bytes 32800 | tf_op jit(solution)/shard_map/ppermute | solution.py:294
  28.4 0.7 %add_add_fusion = f32[128,128]{1,0:T(8,128)} fusion(bf16[128,128]{1,0:T(8,128)(2,1)S(1)} %collective-permute-done.10, bf16[128,128]{1,0:T(8,128)(2,1)S(1)} %collective-permute-done.9, f32[128,128]{1,0:T(8,128)S(1)} %collective-permute-done.8, bf16[128,128]{1,0:T(8,128)(2,1)S(1)} %collective-permute-done.7, bf16[128,128]{1,0:T(8,128)(2,1)S(1)} %get-tuple-element.49), kind=kLoop, calls=%fused_computation.20 | loop fusion | flops 131072 | bytes 262144 | tf_op jit(solution)/shard_map/add | solution.py:419
  (14 shorter events, 0.2 us)
Async XLA Ops:
  5.4 10.4 %copy-start = (bf16[128,2048]{1,0:T(8,128)(2,1)S(1)}, bf16[128,2048]{1,0:T(8,128)(2,1)}, u32[]{:S(2)}) copy-start(bf16[128,2048]{1,0:T(8,128)(2,1)} %refs_2_.1) | copy-start | bytes 1572868
  5.5 7.6 %collective-permute-start = (bf16[3,128,128]{2,1,0:T(8,128)(2,1)S(1)}, bf16[3,128,128]{2,1,0:T(8,128)(2,1)S(1)}, u32[]{:S(2)}, u32[]{:S(2)}) collective-permute-start(bf16[3,128,128]{2,1,0:T(8,128)(2,1)S(1)} %pad_maximum_fusion.2), channel_id=1, source_target_pairs={{0,8},{4,12},{8,0},{12,4},{16,24},{20,28},{24,16},{28,20},{1,9},{5... | collective-permute-start | bytes 294920 | tf_op jit(solution)/shard_map/ppermute | solution.py:294
  8.5 4.5 %collective-permute-start.2 = (bf16[352,128]{1,0:T(8,128)(2,1)S(1)}, bf16[352,128]{1,0:T(8,128)(2,1)S(1)}, u32[]{:S(2)}, u32[]{:S(2)}) collective-permute-start(bf16[352,128]{1,0:T(8,128)(2,1)S(1)} %get-tuple-element.37), channel_id=1, source_target_pairs={{0,16},{4,20},{8,24},{12,28},{16,0},{20,4},{24,8},{28,12},{1,17},{... | collective-permute-start | bytes 270344 | tf_op jit(solution)/shard_map/ppermute | solution.py:294
  13.0 1.3 %collective-permute-start.3 = (bf16[352,128]{1,0:T(8,128)(2,1)S(1)}, bf16[352,128]{1,0:T(8,128)(2,1)S(1)}, u32[]{:S(2)}, u32[]{:S(2)}) collective-permute-start(bf16[352,128]{1,0:T(8,128)(2,1)S(1)} %collective-permute-done.2.mine_ref), channel_id=1, source_target_pairs={{0,4},{4,0},{8,12},{12,8},{16,20},{20,16},{24,28},{28,24},{1,5},{5... | collective-permute-start | bytes 270344 | tf_op jit(solution)/shard_map/ppermute | solution.py:294
  13.1 2.8 %collective-permute-start.1 = (f32[256,128]{1,0:T(8,128)S(1)}, f32[256,128]{1,0:T(8,128)S(1)}, u32[]{:S(2)}, u32[]{:S(2)}) collective-permute-start(f32[256,128]{1,0:T(8,128)S(1)} %pad_maximum_fusion.1.mine_ref), channel_id=1, source_target_pairs={{0,4},{4,0},{8,12},{12,8},{16,20},{20,16},{24,28},{28,24},{1,5},{5... | collective-permute-start | bytes 393224 | tf_op jit(solution)/shard_map/ppermute | solution.py:294
  15.6 5.3 %collective-permute-start.4 = (bf16[3,128,128]{2,1,0:T(8,128)(2,1)S(1)}, bf16[3,128,128]{2,1,0:T(8,128)(2,1)S(1)}, u32[]{:S(2)}, u32[]{:S(2)}) collective-permute-start(bf16[3,128,128]{2,1,0:T(8,128)(2,1)S(1)} %pad_maximum_fusion.3), channel_id=1, source_target_pairs={{0,8},{4,12},{8,0},{12,4},{16,24},{20,28},{24,16},{28,20},{1,9},{5... | collective-permute-start | bytes 294920 | tf_op jit(solution)/shard_map/ppermute | solution.py:294
  15.8 5.8 %collective-permute-start.6 = (bf16[128,2048]{1,0:T(8,128)(2,1)S(1)}, bf16[128,2048]{1,0:T(8,128)(2,1)S(1)}, u32[]{:S(2)}, u32[]{:S(2)}) collective-permute-start(bf16[128,2048]{1,0:T(8,128)(2,1)S(1)} %copy-done), channel_id=1, source_target_pairs={{0,4},{4,0},{8,12},{12,8},{16,20},{20,16},{24,28},{28,24},{1,5},{5... | collective-permute-start | bytes 1572872 | tf_op jit(solution)/shard_map/ppermute | solution.py:294
  16.4 4.9 %collective-permute-start.7 = (bf16[128,128]{1,0:T(8,128)(2,1)S(1)}, bf16[128,128]{1,0:T(8,128)(2,1)S(1)}, u32[]{:S(2)}, u32[]{:S(2)}) collective-permute-start(bf16[128,128]{1,0:T(8,128)(2,1)S(1)} %get-tuple-element.49), channel_id=1, source_target_pairs={{0,8},{4,12},{8,0},{12,4},{16,24},{20,28},{24,16},{28,20},{1,9},{5... | collective-permute-start | bytes 98312 | tf_op jit(solution)/shard_map/ppermute | solution.py:294
  21.0 1.4 %collective-permute-start.5 = (f32[272,128]{1,0:T(8,128)S(1)}, f32[272,128]{1,0:T(8,128)S(1)}, u32[]{:S(2)}, u32[]{:S(2)}) collective-permute-start(f32[272,128]{1,0:T(8,128)S(1)} %pad_maximum_fusion.mine_ref), channel_id=1, source_target_pairs={{0,4},{4,0},{8,12},{12,8},{16,20},{20,16},{24,28},{28,24},{1,5},{5... | collective-permute-start | bytes 417800 | tf_op jit(solution)/shard_map/ppermute | solution.py:294
  21.3 5.2 %collective-permute-start.8 = (f32[128,128]{1,0:T(8,128)S(1)}, f32[128,128]{1,0:T(8,128)S(1)}, u32[]{:S(2)}, u32[]{:S(2)}) collective-permute-start(f32[128,128]{1,0:T(8,128)S(1)} %convert_add_fusion), channel_id=1, source_target_pairs={{0,4},{4,0},{8,12},{12,8},{16,20},{20,16},{24,28},{28,24},{1,5},{5... | collective-permute-start | bytes 196616 | tf_op jit(solution)/shard_map/ppermute | solution.py:294
  23.1 4.9 %collective-permute-start.10 = (bf16[128,128]{1,0:T(8,128)(2,1)S(1)}, bf16[128,128]{1,0:T(8,128)(2,1)S(1)}, u32[]{:S(2)}, u32[]{:S(2)}) collective-permute-start(bf16[128,128]{1,0:T(8,128)(2,1)S(1)} %get-tuple-element.50), channel_id=1, source_target_pairs={{0,24},{4,28},{8,16},{12,20},{16,8},{20,12},{24,0},{28,4},{1,25},{... | collective-permute-start | bytes 98312 | tf_op jit(solution)/shard_map/ppermute | solution.py:294
  24.4 3.9 %collective-permute-start.9 = (bf16[128,128]{1,0:T(8,128)(2,1)S(1)}, bf16[128,128]{1,0:T(8,128)(2,1)S(1)}, u32[]{:S(2)}, u32[]{:S(2)}) collective-permute-start(bf16[128,128]{1,0:T(8,128)(2,1)S(1)} %get-tuple-element.50), channel_id=1, source_target_pairs={{0,16},{4,20},{8,24},{12,28},{16,0},{20,4},{24,8},{28,12},{1,17},{... | collective-permute-start | bytes 98312 | tf_op jit(solution)/shard_map/ppermute | solution.py:294
